TPU v7x, 128 devices: a whole 4x4x4 slice. The times are simulated.
128 devices in a mesh: seq: 32 (over x, y, core), head: 4 (over z).
Axes of the slice: x: 4, y: 4, z: 4, core: 2. Of those that a mesh axis runs over, the one named last changes fastest.
Arguments:
- queries: bfloat16 [8192, 64, 128], P('seq', 'head'), may hold values from -200 to 200
- keys: bfloat16 [8192, 8, 128], P('seq', 'head'), may hold values from -8 to 8
- values: bfloat16 [8192, 8, 128], P('seq', 'head'), may hold values from -6 to 6
- query_map: bfloat16 [64, 128, 64], P('head'), may hold values from -40 to 40
- key_map: bfloat16 [8, 128, 64], P('head'), may hold values from -40 to 40
Outputs:
- teacher_attn: bfloat16 [8192, 64, 128], P('seq', 'head')
- student_attn: bfloat16 [8192, 64, 128], P('seq', 'head')
- loss: float32 [], replicated
All inputs are finite; a program needn't handle non-finite values.
Results may differ from a plain program's by a relative error of at most 0.01.
Values may be sent and summed in bfloat16 or wider, within the bound.
No kernel may reach another device: no remote copies, remote signals or barrier semaphores. Data moves between devices by JAX's collectives and lax.ppermute only.
A program may use at most 320 MiB of HBM per device.

v0:
```python
import jax
import jax.numpy as jnp
import numpy as np
from jax import lax
from jax.experimental import pallas as pl
from jax.experimental.pallas import tpu as pltpu
from jax.sharding import Mesh
from jax.sharding import PartitionSpec as P


SEQ = ("x", "y", "c")
BF = jnp.bfloat16
F32 = jnp.float32
NT = (((1,), (1,)), ((), ()))
BLK = 256
SUB = 1024

OFFSETS = (0, 3, 1, 2)


def slot_table():
    table = np.zeros((16, 2, 16), np.int32)
    for chip in range(16):
        for slot in range(16):
            one, two = OFFSETS[slot % 4], OFFSETS[slot // 4]
            for core, (dx, dy) in enumerate(((one, two), (two, one))):
                table[chip, core, slot] = moved(chip, dx, dy)
    return table


def moved(chip, dx, dy):
    return (chip // 4 + dx) % 4 * 4 + (chip + dy) % 4


TABLE = slot_table()


def permute(value, axes, target):
    pairs = []
    for chip in range(16):
        for core in range(2):
            to = target(chip, core)
            if to is not None:
                pairs.append((chip * 2 + core, to[0] * 2 + to[1]))
    return lax.ppermute(value, axes, pairs)


def features(mapped):
    high = jnp.max(mapped, axis=0, keepdims=True)
    low = jnp.min(mapped, axis=0, keepdims=True)
    up = jnp.exp(mapped - high)
    down = jnp.exp(low - mapped)
    up = up * (1.0 / jnp.sum(up, axis=0, keepdims=True))
    down = down * (1.0 / jnp.sum(down, axis=0, keepdims=True))
    return jnp.concatenate([up, down], axis=0).astype(BF)


def block_at(index, size=BLK):
    return pl.ds(pl.multiple_of(index * size, size), size)


def student_inside(q_ref, keys, values, wk, wq, phi_ref, num_ref, den_ref):
    phi_k = features(lax.dot_general(wk[...], keys, NT, preferred_element_type=F32))
    rows = lax.broadcasted_iota(jnp.int32, (BLK, BLK), 0)
    cols = lax.broadcasted_iota(jnp.int32, (BLK, BLK), 1)

    def head(h, _):
        place = block_at(h)
        mapped = lax.dot_general(wq[h], q_ref[place, :], NT, preferred_element_type=F32)
        phi_q = features(mapped).T
        inner = jnp.dot(phi_q, phi_k, preferred_element_type=F32)
        inner = jnp.where(rows >= cols, inner, 0.0)
        phi_ref[place, :] = phi_q
        num_ref[place, :] = jnp.dot(inner.astype(BF), values, preferred_element_type=F32)
        den_ref[place, :] = inner[:, :128] + inner[:, 128:]
        return 0

    lax.fori_loop(0, 8, head, 0, unroll=2)


def near_kernel(x_ref, kv, wk, wq, phi_ref, num_ref, den_ref):
    student_inside(x_ref, kv[:, :128], kv[:, 128:], wk, wq, phi_ref, num_ref, den_ref)


def add_state(tab, wk, slot, kv, stx, sty, nx, ny):
    chip = tab[16]
    far = 15 - chip
    other = tab[slot]
    ones = jnp.ones((8, BLK), BF)
    phi = features(lax.dot_general(wk[...], kv[:, :128], NT, preferred_element_type=F32))
    phi_a, phi_b = phi[:, :BLK], phi[:, BLK:]
    state_a = jnp.dot(phi_a, kv[:BLK, 128:], preferred_element_type=F32)
    state_b = jnp.dot(phi_b, kv[BLK:, 128:], preferred_element_type=F32)
    norm_a = lax.dot_general(ones, phi_a, NT, preferred_element_type=F32)
    norm_b = lax.dot_general(ones, phi_b, NT, preferred_element_type=F32)
    in_x = jnp.where(other < chip, 1.0, 0.0).astype(F32)
    in_ya = jnp.where(other <= far, 1.0, 0.0).astype(F32)
    in_yb = jnp.where(other < far, 1.0, 0.0).astype(F32)
    stx[...] += in_x * (state_a + state_b)
    nx[...] += in_x * (norm_a + norm_b)
    sty[...] += in_ya * state_a + in_yb * state_b
    ny[...] += in_ya * norm_a + in_yb * norm_b


def far_kernel(tab, y_ref, own, wk, wq, phi_ref, num_ref, den_ref, stx, sty, nx, ny):
    for ref in (stx, sty, nx, ny):
        ref[...] = jnp.zeros_like(ref)
    for i in range(4):
        add_state(tab, wk, i, own[i * 2 * BLK : (i + 1) * 2 * BLK, :], stx, sty, nx, ny)
    keys, values = y_ref[8 * BLK : 9 * BLK, :], y_ref[9 * BLK :, :]
    student_inside(y_ref, keys, values, wk, wq, phi_ref, num_ref, den_ref)


def middle_kernel(tab, left, right, wk, stx0, sty0, nx0, ny0, stx, sty, nx, ny):
    for ref, start in ((stx, stx0), (sty, sty0), (nx, nx0), (ny, ny0)):
        ref[...] = start[...]
    for group, ref in enumerate((left, right)):
        for i in range(4):
            kv = ref[i * 2 * BLK : (i + 1) * 2 * BLK, :]
            add_state(tab, wk, 4 + group * 4 + i, kv, stx, sty, nx, ny)


def finish_kernel(
    tab, opp0, opp1, wk, stx0, sty0, nx0, ny0, phi_x, num_x, den_x, phi_y, num_y, den_y,
    sx_ref, sy_ref, stx, sty, nx, ny,
):
    for ref, start in ((stx, stx0), (sty, sty0), (nx, nx0), (ny, ny0)):
        ref[...] = start[...]
    for group, ref in enumerate((opp0, opp1)):
        for i in range(2):
            kv = ref[i * 2 * BLK : (i + 1) * 2 * BLK, :]
            add_state(tab, wk, 12 + group * 2 + i, kv, stx, sty, nx, ny)
    for phi, num, den, state, norm, out in (
        (phi_x, num_x, den_x, stx, nx, sx_ref),
        (phi_y, num_y, den_y, sty, ny, sy_ref),
    ):
        state_b = state[...].astype(BF)
        norm_row = norm[0:1, :]
        for piece in range(4):
            rows = slice(piece * 512, (piece + 1) * 512)
            phi_q = phi[rows, :]
            top = num[rows, :] + jnp.dot(phi_q, state_b, preferred_element_type=F32)
            low = den[rows, :] + phi_q.astype(F32) * norm_row
            out[rows, :] = (top / jnp.sum(low, axis=-1, keepdims=True)).astype(BF)


def teacher_kernel(
    tab, x_ref, y_ref, own, left, right, opp0, opp1, sx_ref, sy_ref,
    ox_ref, oy_ref, loss_ref, kv_s, part_ref, top_s, sum_s, acc_s, sems,
):
    chip = tab[16]
    far = 15 - chip
    copies = []
    for ref in (own, left, right, opp0, opp1):
        for i in range(ref.shape[0] // (2 * BLK)):
            slot = len(copies)
            copies.append(
                pltpu.make_async_copy(
                    ref.at[pl.ds(i * 2 * BLK, 2 * BLK), :],
                    kv_s.at[block_at(tab[slot], 2 * BLK), :],
                    sems.at[slot],
                )
            )
    for copy in copies:
        copy.start()
    unit = 1.4426950408889634 / 128**0.5
    part_ref[...] = jnp.zeros_like(part_ref)

    def tile(q_ref, piece, k, v, diagonal, first):
        rows = slice(piece * SUB, (piece + 1) * SUB)
        wide = k.shape[0] // 128
        s = lax.dot_general(q_ref[rows, :], k, NT, preferred_element_type=F32) * unit
        if diagonal:
            shape = (SUB, BLK)
            row = lax.broadcasted_iota(jnp.int32, shape, 0) & (BLK - 1)
            last = jnp.where(row >= lax.broadcasted_iota(jnp.int32, shape, 1), s[:, -BLK:], -1e30)
            s = last if wide == 2 else jnp.concatenate([s[:, :-BLK], last], axis=1)
        peak = jnp.broadcast_to(jnp.max(s, axis=-1, keepdims=True), (SUB, 128))
        top = peak if first else jnp.maximum(top_s[rows, :], peak)
        p = jnp.exp2(s - jnp.concatenate([top] * wide, axis=1))
        added = p[:, :128]
        for i in range(1, wide):
            added = added + p[:, i * 128 : (i + 1) * 128]
        mixed = jnp.dot(p.astype(BF), v, preferred_element_type=F32)
        if first:
            sum_s[rows, :] = added
            acc_s[rows, :] = mixed
        else:
            keep = jnp.exp2(top_s[rows, :] - top)
            sum_s[rows, :] = sum_s[rows, :] * keep + added
            acc_s[rows, :] = acc_s[rows, :] * keep + mixed
        top_s[rows, :] = top

    def segment(q_ref, k, v, count, s_ref, o_ref):
        for piece in range(2):
            tile(q_ref, piece, k, v, True, True)

        def step(j, _):
            place = block_at(j, 2 * BLK)
            k, v = kv_s[place, :128], kv_s[place, 128:]
            for piece in range(2):
                tile(q_ref, piece, k, v, False, False)
            return 0

        lax.fori_loop(0, count, step, 0)
        for piece in range(2):
            rows = slice(piece * SUB, (piece + 1) * SUB)
            total = jnp.sum(sum_s[rows, :], axis=-1, keepdims=True)
            out = (acc_s[rows, :] / total).astype(BF)
            o_ref[rows, :] = out
            diff = out.astype(F32) - s_ref[rows, :].astype(F32)
            part_ref[...] += jnp.sum((diff * diff).reshape(SUB // 8, 8, 128), axis=0)

    for copy in copies:
        copy.wait()
    place = block_at(chip * 2)
    segment(x_ref, kv_s[place, :128], kv_s[place, 128:], chip, sx_ref, ox_ref)
    place = block_at(far, 2 * BLK)
    segment(y_ref, kv_s[place, :128], kv_s[place, 128:], far, sy_ref, oy_ref)
    loss_ref[...] = jnp.full_like(loss_ref, jnp.sum(part_ref[...]))


def call(kernel, args, outs, scratch=(), flops=0, table=True, anywhere=(), limit=24):
    vmem = pl.BlockSpec(memory_space=pltpu.VMEM)
    specs = [
        pl.BlockSpec(memory_space=pltpu.SMEM)
        if table and i == 0
        else pl.BlockSpec(memory_space=pl.ANY)
        if i in anywhere
        else vmem
        for i in range(len(args))
    ]
    return pl.pallas_call(
        kernel,
        out_shape=[jax.ShapeDtypeStruct(shape, kind) for shape, kind in outs],
        in_specs=specs,
        out_specs=[vmem] * len(outs),
        scratch_shapes=list(scratch),
        compiler_params=pltpu.CompilerParams(vmem_limit_bytes=limit << 20),
        cost_estimate=pl.CostEstimate(flops=flops, bytes_accessed=1 << 20, transcendentals=0),
    )(*args)


def body(queries, keys, values, query_map, key_map):
    rows, heads, size = queries.shape
    core = lax.axis_index("c")
    chip = lax.axis_index("x") * 4 + lax.axis_index("y")
    first = core == 0
    pick = lambda a, b: jnp.where(first, a, b)

    kv = [jnp.concatenate([keys[:, g], values[:, g]], axis=1) for g in range(2)]
    kv_same, kv_other = pick(kv[0], kv[1]), pick(kv[1], kv[0])
    q = queries.transpose(1, 0, 2).reshape(2, heads // 2 * rows, size)
    q_same, q_other = pick(q[0], q[1]), pick(q[1], q[0])

    kv_came = permute(kv_other, SEQ, lambda r, c: (r, 1 - c))
    q_came = permute(q_other, SEQ, lambda r, c: (r, 1) if c == 0 else None)
    x = pick(q_same, q_came)

    def with_kv(part, pair):
        return jnp.concatenate([part, pair[:, :size], pair[:, size:]], axis=0)

    y_a = permute(
        with_kv(q_other, kv_other), SEQ, lambda r, c: None if c == 0 else (15 - r, 0)
    )
    y_b = permute(
        with_kv(q_same, kv_same), SEQ, lambda r, c: None if c == 0 else (15 - r, 1)
    )
    y = pick(y_a, y_b)
    kv_near = pick(kv_same, kv_came)
    shard = jnp.concatenate([kv_near, pick(kv_came, kv_same)], axis=0)

    def shift(value, phase, by):
        def target(r, c):
            along_x = (c == 0) == (phase == 1)
            return (moved(r, by, 0) if along_x else moved(r, 0, by)), c

        return permute(value, SEQ, target)

    wk = lax.dynamic_index_in_dim(key_map, core, 0, keepdims=False).T
    wq = lax.dynamic_slice_in_dim(query_map, core * 8, 8, 0).transpose(0, 2, 1)
    many = x.shape
    inside = [(many, BF), (many, F32), (many, F32)]
    states = [((128, 128), F32), ((128, 128), F32), ((8, 128), F32), ((8, 128), F32)]

    near_pieces = [shard] + [shift(shard, 1, by) for by in (1, 3, 2)]
    near = call(near_kernel, (x, kv_near, wk, wq), inside, flops=1 << 30, table=False)
    own = jnp.concatenate(near_pieces, axis=0)
    left, right = shift(own, 2, 1), shift(own, 2, 3)
    half = own.shape[0] // 2
    opp0 = shift(left[:half], 2, 1)
    opp1 = shift(right[half:], 2, 3)

    table = lax.dynamic_slice(
        jnp.asarray(TABLE.reshape(32, 16)), (chip * 2 + core, 0), (1, 16)
    ).reshape(16)
    table = jnp.concatenate([table, chip.reshape(1).astype(jnp.int32)])
    *far, stx, sty, nx, ny = call(
        far_kernel, (table, y, own, wk, wq), inside + states, flops=2 << 30
    )
    stx, sty, nx, ny = call(
        middle_kernel, (table, left, right, wk, stx, sty, nx, ny), states, flops=1 << 30
    )
    sx, sy = call(
        finish_kernel,
        (table, opp0, opp1, wk, stx, sty, nx, ny, *near, *far),
        [(many, BF)] * 2,
        [pltpu.VMEM(shape, kind) for shape, kind in states],
        flops=1 << 30,
    )

    def send_back(near, distant):
        came = permute(
            pick(distant, near), SEQ, lambda r, c: (r, 0) if c == 1 else (15 - r, 1)
        )
        came_far = permute(distant, SEQ, lambda r, c: None if c == 0 else (15 - r, 1))
        same = pick(near, came_far)
        return pick(same, came), pick(came, same)

    def assemble(low, high):
        whole = jnp.concatenate([low, high], axis=0).reshape(heads, rows, size)
        return whole.transpose(1, 0, 2)

    student_pair = send_back(sx, sy)
    peers = 32 * lax.axis_size("h")
    ox, oy, part = call(
        teacher_kernel,
        (table, x, y, own, left, right, opp0, opp1, sx, sy),
        [(many, BF), (many, BF), ((peers, 1, 128), F32)],
        [pltpu.VMEM((16 * 2 * BLK, 256), BF), pltpu.VMEM((8, 128), F32)]
        + [pltpu.VMEM((2 * SUB, 128), F32)] * 3
        + [pltpu.SemaphoreType.DMA((16,))],
        flops=9 << 30,
        anywhere=(3, 4, 5, 6, 7),
        limit=32,
    )
    teacher_pair = send_back(ox, oy)

    parts = lax.all_to_all(part, SEQ + ("h",), 0, 0, tiled=True)
    loss = jnp.sum(parts[:, 0, 0]) / (16 * 2 * rows * heads * lax.axis_size("h") * size)
    return assemble(*teacher_pair), assemble(*student_pair), loss


def solution(mesh):
    torus = Mesh(mesh.devices.reshape(4, 4, 2, mesh.shape["head"]), ("x", "y", "c", "h"))
    return jax.shard_map(
        body,
        mesh=torus,
        in_specs=(
            P(SEQ, "h", None),
            P(SEQ, "h", None),
            P(SEQ, "h", None),
            P("h", None, None),
            P("h", None, None),
        ),
        out_specs=(P(SEQ, "h", None), P(SEQ, "h", None), P()),
        check_vma=False,
    )
```

profile of v0, /device:TPU:1, one launch (start us, length us, event | category | flops | bytes accessed | tf_op | source)
XLA Modules:
  0.0 140.5 jit_solution(5101764186679246894)
XLA Ops:
  0.7 1.3 fusion.3
  3.9 1.4 collective-permute-start.3
  7.7 8.0 %collective-permute-start.1 = (bf16[2560,128]{1,0:T(8,128)(2,1)S(1)}, bf16[2560,128]{1,0:T(8,128)(2,1)S(1)}, u32[]{:S(2)}, u32[]{:S(2)}) collective-permute-start(bf16[2560,128]{1,0:T(8,128)(2,1)S(1)} %pad_maximum_fusion.2), channel_id=1, source_target_pairs={{4,120},{12,112},{20,104},{28,96},{36,88},{44,80},{52,72},{60,64},... | collective-permute-start | bytes 1966088 | tf_op jit(solution)/shard_map/ppermute | solution.py:45
  18.7 1.6 %collective-permute-start.5 = (bf16[512,256]{1,0:T(8,128)(2,1)S(1)}, bf16[512,256]{1,0:T(8,128)(2,1)S(1)}, u32[]{:S(2)}, u32[]{:S(2)}) collective-permute-start(bf16[512,256]{1,0:T(8,128)(2,1)S(1)} %pad_maximum_fusion.4), channel_id=1, source_target_pairs={{0,96},{4,28},{8,104},{12,4},{16,112},{20,12},{24,120},{28,20},{32... | collective-permute-start | bytes 786440 | tf_op jit(solution)/shard_map/ppermute | solution.py:45
  20.3 10.0 %collective-permute-done.4 = bf16[512,256]{1,0:T(8,128)(2,1)S(1)} collective-permute-done((bf16[512,256]{1,0:T(8,128)(2,1)S(1)}, bf16[512,256]{1,0:T(8,128)(2,1)S(1)}, u32[]{:S(2)}, u32[]{:S(2)}) %collective-permute-start.4) | collective-permute-done | bytes 262176 | tf_op jit(solution)/shard_map/ppermute | solution.py:45
  30.3 4.4 %collective-permute-done.5 = bf16[512,256]{1,0:T(8,128)(2,1)S(1)} collective-permute-done((bf16[512,256]{1,0:T(8,128)(2,1)S(1)}, bf16[512,256]{1,0:T(8,128)(2,1)S(1)}, u32[]{:S(2)}, u32[]{:S(2)}) %collective-permute-start.5) | collective-permute-done | bytes 262176 | tf_op jit(solution)/shard_map/ppermute | solution.py:45
  34.9 1.5 %collective-permute-start.7 = (bf16[2048,256]{1,0:T(8,128)(2,1)S(1)}, bf16[2048,256]{1,0:T(8,128)(2,1)S(1)}, u32[]{:S(2)}, u32[]{:S(2)}) collective-permute-start(bf16[2048,256]{1,0:T(8,128)(2,1)S(1)} %constant_dynamic-update-slice_fusion.own), channel_id=1, source_target_pairs={{0,8},{4,36},{8,16},{12,44},{16,24},{20,52},{24,0},{28,60},{32,40}... | collective-permute-start | bytes 3145736 | tf_op jit(solution)/shard_map/ppermute | solution.py:45
  36.4 6.3 %collective-permute-start.2 = (bf16[2560,128]{1,0:T(8,128)(2,1)S(1)}, bf16[2560,128]{1,0:T(8,128)(2,1)S(1)}, u32[]{:S(2)}, u32[]{:S(2)}) collective-permute-start(bf16[2560,128]{1,0:T(8,128)(2,1)S(1)} %pad_maximum_fusion.3), channel_id=1, source_target_pairs={{4,124},{12,116},{20,108},{28,100},{36,92},{44,84},{52,76},{60,68}... | collective-permute-start | bytes 1966088 | tf_op jit(solution)/shard_map/ppermute | solution.py:45
  42.9 3.6 %shard_map.87 = (bf16[2048,128]{1,0:T(8,128)(2,1)S(1)}, f32[2048,128]{1,0:T(8,128)S(1)}, f32[2048,128]{1,0:T(8,128)S(1)}) custom-call(bf16[2048,128]{1,0:T(8,128)(2,1)S(1)} %broadcast_select_fusion.11.x_ref, bf16[256,256]{1,0:T(8,128)(2,1)S(1)} %get-tuple-element.44.kv, bf16[64,128]{1,0:T(8,128)(2,1)S(1)} %dynamic-slice_bitcast_fusion.1.wk, ...), custom_call_target="tpu_custom_call" | custom-call | flops 1073741824 | bytes 1048576 | tf_op jit(solution)/shard_map/pallas_call | solution.py:233
  46.5 2.3 %collective-permute-done.8.right = bf16[2048,256]{1,0:T(8,128)(2,1)S(1)} collective-permute-done((bf16[2048,256]{1,0:T(8,128)(2,1)S(1)}, bf16[2048,256]{1,0:T(8,128)(2,1)S(1)}, u32[]{:S(2)}, u32[]{:S(2)}) %collective-permute-start.8) | collective-permute-done | bytes 1048608 | tf_op jit(solution)/shard_map/ppermute | solution.py:45
  50.5 9.6 %collective-permute-done.2 = bf16[2560,128]{1,0:T(8,128)(2,1)S(1)} collective-permute-done((bf16[2560,128]{1,0:T(8,128)(2,1)S(1)}, bf16[2560,128]{1,0:T(8,128)(2,1)S(1)}, u32[]{:S(2)}, u32[]{:S(2)}) %collective-permute-start.2) | collective-permute-done | bytes 655392 | tf_op jit(solution)/shard_map/ppermute | solution.py:45
  60.1 5.2 %shard_map.85 = (bf16[2048,128]{1,0:T(8,128)(2,1)S(1)}, f32[2048,128]{1,0:T(8,128)S(1)}, f32[2048,128]{1,0:T(8,128)S(1)}, f32[128,128]{1,0:T(8,128)S(1)}, f32[12...) custom-call(s32[17]{0:T(128)S(1)} %pad_add_fusion.tab, ...), custom_call_target="tpu_custom_call" | custom-call | flops 2147483648 | bytes 1048576 | tf_op jit(solution)/shard_map/pallas_call | solution.py:233
  65.3 2.9 %shard_map.86 = (f32[128,128]{1,0:T(8,128)S(1)}, f32[128,128]{1,0:T(8,128)S(1)}, f32[8,128]{1,0:T(8,128)S(1)}, f32[8,128]{1,0:T(8,128)S(1)}) custom-call(s32[17]{0:T(128)S(1)} %pad_add_fusion.tab, bf16[2048,256]{1,0:T(8,128)(2,1)S(1)} %collective-permute-done.7.left, bf16[2048,256]{1,0:T(8,128)(2,1)S(1)} %collective-permute-done.8.right, ...), custom_call_target="tpu_custom_call" | custom-call | flops 1073741824 | bytes 1048576 | tf_op jit(solution)/shard_map/pallas_call | solution.py:233
  68.2 2.5 %shard_map.88 = (bf16[2048,128]{1,0:T(8,128)(2,1)S(1)}, bf16[2048,128]{1,0:T(8,128)(2,1)S(1)}) custom-call(s32[17]{0:T(128)S(1)} %pad_add_fusion.tab, bf16[1024,256]{1,0:T(8,128)(2,1)S(1)} %collective-permute-done.9.opp0, bf16[1024,256]{1,0:T(8,128)(2,1)S(1)} %collective-permute-done.10.opp1, bf16[64,128]{1,0:T(8,128)(2,1)S(1)} %dynamic-slice_bitcast_fusion.1.wk, ...), custom_call_target="tpu_custom_call" | custom-call | flops 1073741824 | bytes 1048576 | tf_op jit(solution)/shard_map/pallas_call | solution.py:233
  70.7 30.1 %shard_map.89 = (bf16[2048,128]{1,0:T(8,128)(2,1)S(1)}, bf16[2048,128]{1,0:T(8,128)(2,1)S(1)}, f32[128,1,128]{2,1,0:T(1,128)}) custom-call(s32[17]{0:T(128)S(1)} %pad_add_fusion.tab, bf16[2048,128]{1,0:T(8,128)(2,1)S(1)} %broadcast_select_fusion.11.x_ref, bf16[2560,128]{1,0:T(8,128)(2,1)S(1)} %broadcast_select_fusion.y_ref, ...), custom_call_target="tpu_custom_call" | custom-call | flops 9663676416 | bytes 1048576 | tf_op jit(solution)/shard_map/pallas_call | solution.py:233
  100.9 5.2 %all-to-all-start = ((f32[128,1,128]{2,1,0:T(1,128)}), f32[128,1,128]{2,1,0:T(1,128)S(1)}, u32[]{:S(2)}, u32[]{:S(2)}) async-start(f32[128,1,128]{2,1,0:T(1,128)} %get-tuple-element.40), calls=%async_computation | async-start | bytes 131072 | tf_op jit(solution)/shard_map/all_to_all | solution.py:339
  106.1 6.7 %collective-permute-start.11 = (bf16[2048,128]{1,0:T(8,128)(2,1)S(1)}, bf16[2048,128]{1,0:T(8,128)(2,1)}, u32[]{:S(2)}, u32[]{:S(2)}) collective-permute-start(bf16[2048,128]{1,0:T(8,128)(2,1)S(1)} %get-tuple-element.39), channel_id=1, source_target_pairs={{4,124},{12,116},{20,108},{28,100},{36,92},{44,84},{52,76},{60,68}... | collective-permute-start | bytes 1572872 | tf_op jit(solution)/shard_map/ppermute | solution.py:45
  113.0 1.9 %collective-permute-start.13 = (bf16[2048,128]{1,0:T(8,128)(2,1)S(1)}, bf16[2048,128]{1,0:T(8,128)(2,1)}, u32[]{:S(2)}, u32[]{:S(2)}) collective-permute-start(bf16[2048,128]{1,0:T(8,128)(2,1)S(1)} %get-tuple-element.37.sy_ref), channel_id=1, source_target_pairs={{4,124},{12,116},{20,108},{28,100},{36,92},{44,84},{52,76},{60,68}... | collective-permute-start | bytes 1572872 | tf_op jit(solution)/shard_map/ppermute | solution.py:45
  117.2 12.3 %collective-permute-done.12 = bf16[2048,128]{1,0:T(8,128)(2,1)} collective-permute-done((bf16[2048,128]{1,0:T(8,128)(2,1)S(1)}, bf16[2048,128]{1,0:T(8,128)(2,1)}, u32[]{:S(2)}, u32[]{:S(2)}) %collective-permute-start.12) | collective-permute-done | bytes 524320 | tf_op jit(solution)/shard_map/ppermute | solution.py:45
  129.4 1.3 broadcast_select_fusion.8
  130.8 1.6 %copy.28 = bf16[16,256,128]{2,0,1:T(8,128)(2,1)} copy(bf16[16,256,128]{2,1,0:T(8,128)(2,1)S(1)} %bitcast.30) | data formatting | bytes 2097152 | tf_op jit(solution)/shard_map/reshape | solution.py:321
  132.5 3.9 %collective-permute-done.14 = bf16[2048,128]{1,0:T(8,128)(2,1)} collective-permute-done((bf16[2048,128]{1,0:T(8,128)(2,1)S(1)}, bf16[2048,128]{1,0:T(8,128)(2,1)}, u32[]{:S(2)}, u32[]{:S(2)}) %collective-permute-start.14) | collective-permute-done | bytes 524320 | tf_op jit(solution)/shard_map/ppermute | solution.py:45
  136.3 1.3 broadcast_select_fusion.4
  137.7 1.6 %copy.27 = bf16[16,256,128]{2,0,1:T(8,128)(2,1)} copy(bf16[16,256,128]{2,1,0:T(8,128)(2,1)S(1)} %bitcast.31) | data formatting | bytes 2097152 | tf_op jit(solution)/shard_map/reshape | solution.py:321
  (52 shorter events, 11.2 us)
Async XLA Ops:
  0.6 15.8 %copy-start = (bf16[16,128,64]{1,2,0:T(8,128)(2,1)S(1)}, bf16[16,128,64]{1,2,0:T(8,128)(2,1)}, u32[]{:S(2)}) copy-start(bf16[16,128,64]{1,2,0:T(8,128)(2,1)} %param.9) | copy-start | bytes 786436
  0.7 4.7 %copy-start.1 = (bf16[256,16,128]{2,1,0:T(8,128)(2,1)S(1)}, bf16[256,16,128]{2,1,0:T(8,128)(2,1)}, u32[]{:S(2)}) copy-start(bf16[256,16,128]{2,1,0:T(8,128)(2,1)} %param.6) | copy-start | bytes 3145732
  3.9 12.6 %collective-permute-start.3 = (bf16[256,256]{1,0:T(8,128)(2,1)}, bf16[256,256]{1,0:T(8,128)(2,1)S(1)}, u32[]{:S(2)}, u32[]{:S(2)}) collective-permute-start(bf16[256,256]{1,0:T(8,128)(2,1)} %broadcast_select_fusion.15), channel_id=1, source_target_pairs={{0,4},{4,0},{8,12},{12,8},{16,20},{20,16},{24,28},{28,24},{32,36},... | collective-permute-start | bytes 393224 | tf_op jit(solution)/shard_map/ppermute | solution.py:45
  5.5 37.3 %collective-permute-start = (bf16[2048,128]{1,0:T(8,128)(2,1)S(1)}, bf16[2048,128]{1,0:T(8,128)(2,1)S(1)}, u32[]{:S(2)}, u32[]{:S(2)}) collective-permute-start(bf16[2048,128]{1,0:T(8,128)(2,1)S(1)} %bitcast.32), channel_id=1, source_target_pairs={{0,4},{8,12},{16,20},{24,28},{32,36},{40,44},{48,52},{56,60},{64,6... | collective-permute-start | bytes 1572872 | tf_op jit(solution)/shard_map/ppermute | solution.py:45
  7.7 42.8 %collective-permute-start.1 = (bf16[2560,128]{1,0:T(8,128)(2,1)S(1)}, bf16[2560,128]{1,0:T(8,128)(2,1)S(1)}, u32[]{:S(2)}, u32[]{:S(2)}) collective-permute-start(bf16[2560,128]{1,0:T(8,128)(2,1)S(1)} %pad_maximum_fusion.2), channel_id=1, source_target_pairs={{4,120},{12,112},{20,104},{28,96},{36,88},{44,80},{52,72},{60,64},... | collective-permute-start | bytes 1966088 | tf_op jit(solution)/shard_map/ppermute | solution.py:45
  16.6 13.7 %collective-permute-start.4 = (bf16[512,256]{1,0:T(8,128)(2,1)S(1)}, bf16[512,256]{1,0:T(8,128)(2,1)S(1)}, u32[]{:S(2)}, u32[]{:S(2)}) collective-permute-start(bf16[512,256]{1,0:T(8,128)(2,1)S(1)} %pad_maximum_fusion.4), channel_id=1, source_target_pairs={{0,32},{4,12},{8,40},{12,20},{16,48},{20,28},{24,56},{28,4},{32,64... | collective-permute-start | bytes 786440 | tf_op jit(solution)/shard_map/ppermute | solution.py:45
  17.5 17.3 %collective-permute-start.6 = (bf16[512,256]{1,0:T(8,128)(2,1)S(1)}, bf16[512,256]{1,0:T(8,128)(2,1)S(1)}, u32[]{:S(2)}, u32[]{:S(2)}) collective-permute-start(bf16[512,256]{1,0:T(8,128)(2,1)S(1)} %pad_maximum_fusion.4), channel_id=1, source_target_pairs={{0,64},{4,20},{8,72},{12,28},{16,80},{20,4},{24,88},{28,12},{32,96... | collective-permute-start | bytes 786440 | tf_op jit(solution)/shard_map/ppermute | solution.py:45
  18.7 16.1 %collective-permute-start.5 = (bf16[512,256]{1,0:T(8,128)(2,1)S(1)}, bf16[512,256]{1,0:T(8,128)(2,1)S(1)}, u32[]{:S(2)}, u32[]{:S(2)}) collective-permute-start(bf16[512,256]{1,0:T(8,128)(2,1)S(1)} %pad_maximum_fusion.4), channel_id=1, source_target_pairs={{0,96},{4,28},{8,104},{12,4},{16,112},{20,12},{24,120},{28,20},{32... | collective-permute-start | bytes 786440 | tf_op jit(solution)/shard_map/ppermute | solution.py:45
  34.8 14.0 %collective-permute-start.8 = (bf16[2048,256]{1,0:T(8,128)(2,1)S(1)}, bf16[2048,256]{1,0:T(8,128)(2,1)S(1)}, u32[]{:S(2)}, u32[]{:S(2)}) collective-permute-start(bf16[2048,256]{1,0:T(8,128)(2,1)S(1)} %constant_dynamic-update-slice_fusion.own), channel_id=1, source_target_pairs={{0,24},{4,100},{8,0},{12,108},{16,8},{20,116},{24,16},{28,124},{32... | collective-permute-start | bytes 3145736 | tf_op jit(solution)/shard_map/ppermute | solution.py:45
  34.9 15.0 %collective-permute-start.7 = (bf16[2048,256]{1,0:T(8,128)(2,1)S(1)}, bf16[2048,256]{1,0:T(8,128)(2,1)S(1)}, u32[]{:S(2)}, u32[]{:S(2)}) collective-permute-start(bf16[2048,256]{1,0:T(8,128)(2,1)S(1)} %constant_dynamic-update-slice_fusion.own), channel_id=1, source_target_pairs={{0,8},{4,36},{8,16},{12,44},{16,24},{20,52},{24,0},{28,60},{32,40}... | collective-permute-start | bytes 3145736 | tf_op jit(solution)/shard_map/ppermute | solution.py:45
  36.4 23.7 %collective-permute-start.2 = (bf16[2560,128]{1,0:T(8,128)(2,1)S(1)}, bf16[2560,128]{1,0:T(8,128)(2,1)S(1)}, u32[]{:S(2)}, u32[]{:S(2)}) collective-permute-start(bf16[2560,128]{1,0:T(8,128)(2,1)S(1)} %pad_maximum_fusion.3), channel_id=1, source_target_pairs={{4,124},{12,116},{20,108},{28,100},{36,92},{44,84},{52,76},{60,68}... | collective-permute-start | bytes 1966088 | tf_op jit(solution)/shard_map/ppermute | solution.py:45
  48.9 19.3 %collective-permute-start.10 = (bf16[1024,256]{1,0:T(8,128)(2,1)S(1)}, bf16[1024,256]{1,0:T(8,128)(2,1)S(1)}, u32[]{:S(2)}, u32[]{:S(2)}) collective-permute-start(bf16[1024,256]{1,0:T(8,128)(2,1)S(1)} %slice.63), channel_id=1, source_target_pairs={{0,24},{4,100},{8,0},{12,108},{16,8},{20,116},{24,16},{28,124},{32... | collective-permute-start | bytes 1572872 | tf_op jit(solution)/shard_map/ppermute | solution.py:45
  49.9 18.3 %collective-permute-start.9 = (bf16[1024,256]{1,0:T(8,128)(2,1)S(1)}, bf16[1024,256]{1,0:T(8,128)(2,1)S(1)}, u32[]{:S(2)}, u32[]{:S(2)}) collective-permute-start(bf16[1024,256]{1,0:T(8,128)(2,1)S(1)} %slice.62), channel_id=1, source_target_pairs={{0,8},{4,36},{8,16},{12,44},{16,24},{20,52},{24,0},{28,60},{32,40}... | collective-permute-start | bytes 1572872 | tf_op jit(solution)/shard_map/ppermute | solution.py:45
  100.9 14.9 %all-to-all-start = ((f32[128,1,128]{2,1,0:T(1,128)}), f32[128,1,128]{2,1,0:T(1,128)S(1)}, u32[]{:S(2)}, u32[]{:S(2)}) async-start(f32[128,1,128]{2,1,0:T(1,128)} %get-tuple-element.40), calls=%async_computation | async-start | bytes 131072 | tf_op jit(solution)/shard_map/all_to_all | solution.py:339
  106.1 23.3 %collective-permute-start.11 = (bf16[2048,128]{1,0:T(8,128)(2,1)S(1)}, bf16[2048,128]{1,0:T(8,128)(2,1)}, u32[]{:S(2)}, u32[]{:S(2)}) collective-permute-start(bf16[2048,128]{1,0:T(8,128)(2,1)S(1)} %get-tuple-element.39), channel_id=1, source_target_pairs={{4,124},{12,116},{20,108},{28,100},{36,92},{44,84},{52,76},{60,68}... | collective-permute-start | bytes 1572872 | tf_op jit(solution)/shard_map/ppermute | solution.py:45
  112.9 16.5 %collective-permute-start.12 = (bf16[2048,128]{1,0:T(8,128)(2,1)S(1)}, bf16[2048,128]{1,0:T(8,128)(2,1)}, u32[]{:S(2)}, u32[]{:S(2)}) collective-permute-start(bf16[2048,128]{1,0:T(8,128)(2,1)S(1)} %broadcast_select_fusion.9), channel_id=1, source_target_pairs={{0,124},{4,0},{8,116},{12,8},{16,108},{20,16},{24,100},{28,24},{32... | collective-permute-start | bytes 1572872 | tf_op jit(solution)/shard_map/ppermute | solution.py:45
  113.0 23.3 %collective-permute-start.13 = (bf16[2048,128]{1,0:T(8,128)(2,1)S(1)}, bf16[2048,128]{1,0:T(8,128)(2,1)}, u32[]{:S(2)}, u32[]{:S(2)}) collective-permute-start(bf16[2048,128]{1,0:T(8,128)(2,1)S(1)} %get-tuple-element.37.sy_ref), channel_id=1, source_target_pairs={{4,124},{12,116},{20,108},{28,100},{36,92},{44,84},{52,76},{60,68}... | collective-permute-start | bytes 1572872 | tf_op jit(solution)/shard_map/ppermute | solution.py:45
  115.0 21.4 %collective-permute-start.14 = (bf16[2048,128]{1,0:T(8,128)(2,1)S(1)}, bf16[2048,128]{1,0:T(8,128)(2,1)}, u32[]{:S(2)}, u32[]{:S(2)}) collective-permute-start(bf16[2048,128]{1,0:T(8,128)(2,1)S(1)} %broadcast_select_fusion.5), channel_id=1, source_target_pairs={{0,124},{4,0},{8,116},{12,8},{16,108},{20,16},{24,100},{28,24},{32... | collective-permute-start | bytes 1572872 | tf_op jit(solution)/shard_map/ppermute | solution.py:45
where the time goes:
time: 141 us
  Pallas kernels  44.3 us (31%)
  waiting for transfers between devices  43.1 us (31%)
  starting transfers between devices  37.1 us (26%)
  local copies, waits for them, and re-layouts  8.45 us (6%)
  other arithmetic  4.78 us (3%)
  between operations  2.75 us (2%)
    pallas_call x5, Pallas kernels, call(): pl.pallas_call(kernel, out_shape=[jax.ShapeDtypeStruct(shape, kind) for s...  44.3 us
    ppermute x15, waiting for transfers between devices, permute(): return lax.ppermute(value, axes, pairs)  42.4 us
    ppermute x15, starting transfers between devices, permute(): return lax.ppermute(value, axes, pairs)  31.8 us
    all_to_all x1, starting transfers between devices, body(): parts = lax.all_to_all(part, SEQ + ('h',), 0, 0, tiled=True)  5.24 us
    select_n x8, other arithmetic, body(): pick = lambda a, b: jnp.where(first, a, b)  3.63 us
    reshape x2, local copies, waits for them, and re-layouts, assemble(): whole = jnp.concatenate([low, high], axis=0).reshape(heads, rows, size)  3.3 us
  transfers between devices with their start and end apart: 16, of which 7 were waited for; matrix products, arithmetic and copies ran while one was open for 5% of the time, Pallas kernels for 8%

commit v1 on v0

--- a/solution.py
+++ b/solution.py
@@ -15,21 +15,21 @@
 BLK = 256
 SUB = 1024
 
-OFFSETS = (0, 3, 1, 2)
+MASKS = (0, 1, 3, 2)
+
+
+def moved(chip, mx, my):
+    return chip ^ (mx * 4 + my)
 
 
 def slot_table():
     table = np.zeros((16, 2, 16), np.int32)
     for chip in range(16):
         for slot in range(16):
-            one, two = OFFSETS[slot % 4], OFFSETS[slot // 4]
-            for core, (dx, dy) in enumerate(((one, two), (two, one))):
-                table[chip, core, slot] = moved(chip, dx, dy)
+            one, two = MASKS[slot % 4], MASKS[slot // 4]
+            for core, (mx, my) in enumerate(((one, two), (two, one))):
+                table[chip, core, slot] = moved(chip, mx, my)
     return table
-
-
-def moved(chip, dx, dy):
-    return (chip // 4 + dx) % 4 * 4 + (chip + dy) % 4
 
 
 TABLE = slot_table()
@@ -59,27 +59,25 @@
     return pl.ds(pl.multiple_of(index * size, size), size)
 
 
-def student_inside(q_ref, keys, values, wk, wq, phi_ref, num_ref, den_ref):
+def student_inside(q_ref, keys, values, wk, wq, phi_ref, num_ref, den_ref, wide_s):
+    wide_s[...] = q_ref[: 8 * BLK, :].astype(F32)
     phi_k = features(lax.dot_general(wk[...], keys, NT, preferred_element_type=F32))
     rows = lax.broadcasted_iota(jnp.int32, (BLK, BLK), 0)
     cols = lax.broadcasted_iota(jnp.int32, (BLK, BLK), 1)
 
     def head(h, _):
-        place = block_at(h)
-        mapped = lax.dot_general(wq[h], q_ref[place, :], NT, preferred_element_type=F32)
+        place = pl.ds(h, BLK, stride=8)
+        q = wide_s[place, :].astype(BF)
+        mapped = lax.dot_general(wq[h], q, NT, preferred_element_type=F32)
         phi_q = features(mapped).T
         inner = jnp.dot(phi_q, phi_k, preferred_element_type=F32)
         inner = jnp.where(rows >= cols, inner, 0.0)
-        phi_ref[place, :] = phi_q
+        phi_ref[place, :] = phi_q.astype(F32)
         num_ref[place, :] = jnp.dot(inner.astype(BF), values, preferred_element_type=F32)
         den_ref[place, :] = inner[:, :128] + inner[:, 128:]
         return 0
 
     lax.fori_loop(0, 8, head, 0, unroll=2)
-
-
-def near_kernel(x_ref, kv, wk, wq, phi_ref, num_ref, den_ref):
-    student_inside(x_ref, kv[:, :128], kv[:, 128:], wk, wq, phi_ref, num_ref, den_ref)
 
 
 def add_state(tab, wk, slot, kv, stx, sty, nx, ny):
@@ -102,16 +100,24 @@
     ny[...] += in_ya * norm_a + in_yb * norm_b
 
 
-def far_kernel(tab, y_ref, own, wk, wq, phi_ref, num_ref, den_ref, stx, sty, nx, ny):
+def near_kernel(
+    tab, x_ref, own, wk, wq, phi_ref, num_ref, den_ref, stx, sty, nx, ny, wide_s
+):
     for ref in (stx, sty, nx, ny):
         ref[...] = jnp.zeros_like(ref)
     for i in range(4):
         add_state(tab, wk, i, own[i * 2 * BLK : (i + 1) * 2 * BLK, :], stx, sty, nx, ny)
-    keys, values = y_ref[8 * BLK : 9 * BLK, :], y_ref[9 * BLK :, :]
-    student_inside(y_ref, keys, values, wk, wq, phi_ref, num_ref, den_ref)
-
-
-def middle_kernel(tab, left, right, wk, stx0, sty0, nx0, ny0, stx, sty, nx, ny):
+    keys, values = own[:BLK, :128], own[:BLK, 128:]
+    student_inside(x_ref, keys, values, wk, wq, phi_ref, num_ref, den_ref, wide_s)
+
+
+def far_kernel(
+    tab, y_ref, left, right, wk, wq, stx0, sty0, nx0, ny0,
+    phi_ref, num_ref, den_ref, stx, sty, nx, ny, wide_s,
+):
+    own = slice(5 * BLK, 6 * BLK)
+    keys, values = right[own, :128], right[own, 128:]
+    student_inside(y_ref, keys, values, wk, wq, phi_ref, num_ref, den_ref, wide_s)
     for ref, start in ((stx, stx0), (sty, sty0), (nx, nx0), (ny, ny0)):
         ref[...] = start[...]
     for group, ref in enumerate((left, right)):
@@ -139,8 +145,9 @@
         for piece in range(4):
             rows = slice(piece * 512, (piece + 1) * 512)
             phi_q = phi[rows, :]
-            top = num[rows, :] + jnp.dot(phi_q, state_b, preferred_element_type=F32)
-            low = den[rows, :] + phi_q.astype(F32) * norm_row
+            mixed = jnp.dot(phi_q.astype(BF), state_b, preferred_element_type=F32)
+            top = num[rows, :] + mixed
+            low = den[rows, :] + phi_q * norm_row
             out[rows, :] = (top / jnp.sum(low, axis=-1, keepdims=True)).astype(BF)
 
 
@@ -172,7 +179,7 @@
         s = lax.dot_general(q_ref[rows, :], k, NT, preferred_element_type=F32) * unit
         if diagonal:
             shape = (SUB, BLK)
-            row = lax.broadcasted_iota(jnp.int32, shape, 0) & (BLK - 1)
+            row = (lax.broadcasted_iota(jnp.int32, shape, 0) >> 3) + piece * (SUB // 8)
             last = jnp.where(row >= lax.broadcasted_iota(jnp.int32, shape, 1), s[:, -BLK:], -1e30)
             s = last if wide == 2 else jnp.concatenate([s[:, :-BLK], last], axis=1)
         peak = jnp.broadcast_to(jnp.max(s, axis=-1, keepdims=True), (SUB, 128))
@@ -220,11 +227,29 @@
     loss_ref[...] = jnp.full_like(loss_ref, jnp.sum(part_ref[...]))
 
 
-def call(kernel, args, outs, scratch=(), flops=0, table=True, anywhere=(), limit=24):
+def assemble_kernel(tab, *refs):
+    sources, outs, sems = (refs[:3], refs[3:6]), refs[6:8], refs[8]
+    for core in range(2):
+
+        @pl.when(tab[17] == core)
+        def _(core=core):
+            copies = []
+            for k, ((near, came, distant), out) in enumerate(zip(sources, outs)):
+                halves = (near, came) if core == 0 else (came, distant)
+                for half, source in enumerate(halves):
+                    target = out.at[:, pl.ds(half * 8, 8), :]
+                    copies.append(pltpu.make_async_copy(source, target, sems.at[k * 2 + half]))
+            for copy in copies:
+                copy.start()
+            for copy in copies:
+                copy.wait()
+
+
+def call(kernel, args, outs, scratch=(), flops=0, anywhere=(), limit=24, out_space=pltpu.VMEM):
     vmem = pl.BlockSpec(memory_space=pltpu.VMEM)
     specs = [
         pl.BlockSpec(memory_space=pltpu.SMEM)
-        if table and i == 0
+        if i == 0
         else pl.BlockSpec(memory_space=pl.ANY)
         if i in anywhere
         else vmem
@@ -234,7 +259,7 @@
         kernel,
         out_shape=[jax.ShapeDtypeStruct(shape, kind) for shape, kind in outs],
         in_specs=specs,
-        out_specs=[vmem] * len(outs),
+        out_specs=[pl.BlockSpec(memory_space=out_space)] * len(outs),
         scratch_shapes=list(scratch),
         compiler_params=pltpu.CompilerParams(vmem_limit_bytes=limit << 20),
         cost_estimate=pl.CostEstimate(flops=flops, bytes_accessed=1 << 20, transcendentals=0),
@@ -250,25 +275,16 @@
 
     kv = [jnp.concatenate([keys[:, g], values[:, g]], axis=1) for g in range(2)]
     kv_same, kv_other = pick(kv[0], kv[1]), pick(kv[1], kv[0])
-    q = queries.transpose(1, 0, 2).reshape(2, heads // 2 * rows, size)
-    q_same, q_other = pick(q[0], q[1]), pick(q[1], q[0])
-
     kv_came = permute(kv_other, SEQ, lambda r, c: (r, 1 - c))
+    shard = jnp.concatenate([pick(kv_same, kv_came), pick(kv_came, kv_same)], axis=0)
+
+    q = [queries[:, g * 8 : g * 8 + 8].reshape(8 * rows, size) for g in range(2)]
+    q_same, q_other = lax.optimization_barrier((pick(q[0], q[1]), pick(q[1], q[0])))
+    y_a = permute(q_other, SEQ, lambda r, c: None if c == 0 else (15 - r, 0))
+    y_b = permute(q_same, SEQ, lambda r, c: None if c == 0 else (15 - r, 1))
     q_came = permute(q_other, SEQ, lambda r, c: (r, 1) if c == 0 else None)
     x = pick(q_same, q_came)
-
-    def with_kv(part, pair):
-        return jnp.concatenate([part, pair[:, :size], pair[:, size:]], axis=0)
-
-    y_a = permute(
-        with_kv(q_other, kv_other), SEQ, lambda r, c: None if c == 0 else (15 - r, 0)
-    )
-    y_b = permute(
-        with_kv(q_same, kv_same), SEQ, lambda r, c: None if c == 0 else (15 - r, 1)
-    )
     y = pick(y_a, y_b)
-    kv_near = pick(kv_same, kv_came)
-    shard = jnp.concatenate([kv_near, pick(kv_came, kv_same)], axis=0)
 
     def shift(value, phase, by):
         def target(r, c):
@@ -280,26 +296,31 @@
     wk = lax.dynamic_index_in_dim(key_map, core, 0, keepdims=False).T
     wq = lax.dynamic_slice_in_dim(query_map, core * 8, 8, 0).transpose(0, 2, 1)
     many = x.shape
-    inside = [(many, BF), (many, F32), (many, F32)]
+    inside = [(many, F32)] * 3
+    wide = [pltpu.VMEM(many, F32)]
     states = [((128, 128), F32), ((128, 128), F32), ((8, 128), F32), ((8, 128), F32)]
 
-    near_pieces = [shard] + [shift(shard, 1, by) for by in (1, 3, 2)]
-    near = call(near_kernel, (x, kv_near, wk, wq), inside, flops=1 << 30, table=False)
+    beside, across = shift(shard, 1, 1), shift(shard, 1, 3)
+    near_pieces = [shard, beside, across, shift(across, 1, 1)]
     own = jnp.concatenate(near_pieces, axis=0)
     left, right = shift(own, 2, 1), shift(own, 2, 3)
     half = own.shape[0] // 2
-    opp0 = shift(left[:half], 2, 1)
-    opp1 = shift(right[half:], 2, 3)
+    opp0 = shift(right[:half], 2, 1)
+    opp1 = shift(left[half:], 2, 3)
 
     table = lax.dynamic_slice(
         jnp.asarray(TABLE.reshape(32, 16)), (chip * 2 + core, 0), (1, 16)
     ).reshape(16)
-    table = jnp.concatenate([table, chip.reshape(1).astype(jnp.int32)])
+    table = jnp.concatenate([table, jnp.stack([chip, core]).astype(jnp.int32)])
+    *near, stx, sty, nx, ny = call(
+        near_kernel, (table, x, own, wk, wq), inside + states, wide, 2 << 30
+    )
     *far, stx, sty, nx, ny = call(
-        far_kernel, (table, y, own, wk, wq), inside + states, flops=2 << 30
-    )
-    stx, sty, nx, ny = call(
-        middle_kernel, (table, left, right, wk, stx, sty, nx, ny), states, flops=1 << 30
+        far_kernel,
+        (table, y, left, right, wk, wq, stx, sty, nx, ny),
+        inside + states,
+        wide,
+        2 << 30,
     )
     sx, sy = call(
         finish_kernel,
@@ -314,19 +335,14 @@
             pick(distant, near), SEQ, lambda r, c: (r, 0) if c == 1 else (15 - r, 1)
         )
         came_far = permute(distant, SEQ, lambda r, c: None if c == 0 else (15 - r, 1))
-        same = pick(near, came_far)
-        return pick(same, came), pick(came, same)
-
-    def assemble(low, high):
-        whole = jnp.concatenate([low, high], axis=0).reshape(heads, rows, size)
-        return whole.transpose(1, 0, 2)
-
-    student_pair = send_back(sx, sy)
+        return came, came_far
+
+    student_parts = (sx, *send_back(sx, sy))
     peers = 32 * lax.axis_size("h")
     ox, oy, part = call(
         teacher_kernel,
         (table, x, y, own, left, right, opp0, opp1, sx, sy),
-        [(many, BF), (many, BF), ((peers, 1, 128), F32)],
+        [(many, BF)] * 2 + [((peers, 1, 128), F32)],
         [pltpu.VMEM((16 * 2 * BLK, 256), BF), pltpu.VMEM((8, 128), F32)]
         + [pltpu.VMEM((2 * SUB, 128), F32)] * 3
         + [pltpu.SemaphoreType.DMA((16,))],
@@ -334,11 +350,19 @@
         anywhere=(3, 4, 5, 6, 7),
         limit=32,
     )
-    teacher_pair = send_back(ox, oy)
+    teacher_parts = (ox, *send_back(ox, oy))
 
     parts = lax.all_to_all(part, SEQ + ("h",), 0, 0, tiled=True)
     loss = jnp.sum(parts[:, 0, 0]) / (16 * 2 * rows * heads * lax.axis_size("h") * size)
-    return assemble(*teacher_pair), assemble(*student_pair), loss
+    parts = [p.reshape(rows, 8, size) for p in teacher_parts + student_parts]
+    teacher_attn, student_attn = call(
+        assemble_kernel,
+        (table, *parts),
+        [((rows, heads, size), BF)] * 2,
+        [pltpu.SemaphoreType.DMA((4,))],
+        out_space=pl.ANY,
+    )
+    return teacher_attn, student_attn, loss
 
 
 def solution(mesh):

time: 141 us -> 130 us (0.922)
  waiting for transfers between devices: 43.1 us -> 16.7 us
  blocking collectives: 0 us -> 18.6 us
  local copies, waits for them, and re-layouts: 8.45 us -> 2.39 us
  Pallas kernels: 44.3 us -> 46.5 us
    ppermute x15, waiting for transfers between devices: 42.4 us -> 16.7 us  [permute(): return lax.ppermute(value, axes, pairs)]
    all_to_all x0 -> x1, blocking collectives: none -> 18.6 us  [body(): parts = lax.all_to_all(part, SEQ + ('h',), 0, 0, tiled=True)]
    all_to_all x1 -> x0, starting transfers between devices: 5.24 us -> none  [body(): parts = lax.all_to_all(part, SEQ + ('h',), 0, 0, tiled=True)]
    ppermute x15, starting transfers between devices: 31.8 us -> 36.9 us  [permute(): return lax.ppermute(value, axes, pairs)]
    reshape x2 -> x0, local copies, waits for them, and re-layouts: 3.3 us -> none  [assemble(): whole = jnp.concatenate([low, high], axis=0).reshape(heads, rows, size)]
    pallas_call x5, Pallas kernels: 44.3 us -> 46.5 us  [call(): pl.pallas_call(kernel, out_shape=[jax.ShapeDtypeStruct(shape, kind) for s...]
    select_n x8 -> x6, other arithmetic: 3.63 us -> 4.99 us  [body(): pick = lambda a, b: jnp.where(first, a, b)]
  transfers between devices with their start and end apart: 16 -> 15, of which waited for: 7 -> 5; matrix products, arithmetic and copies ran while one was open for 5% -> 4% of each run, Pallas kernels for 8% -> 32%
where the time goes in v1:
time: 130 us
  Pallas kernels  46.5 us (36%)
  starting transfers between devices  36.9 us (28%)
  blocking collectives  18.6 us (14%)
  waiting for transfers between devices  16.7 us (13%)
  other arithmetic  5.93 us (5%)
  between operations  2.79 us (2%)
  local copies, waits for them, and re-layouts  2.39 us (2%)
    pallas_call x5, Pallas kernels, call(): pl.pallas_call(kernel, out_shape=[jax.ShapeDtypeStruct(shape, kind) for s...  46.5 us
    ppermute x15, starting transfers between devices, permute(): return lax.ppermute(value, axes, pairs)  36.9 us
    all_to_all x1, blocking collectives, body(): parts = lax.all_to_all(part, SEQ + ('h',), 0, 0, tiled=True)  18.6 us
    ppermute x15, waiting for transfers between devices, permute(): return lax.ppermute(value, axes, pairs)  16.7 us
    select_n x6, other arithmetic, body(): pick = lambda a, b: jnp.where(first, a, b)  4.99 us
  transfers between devices with their start and end apart: 15, of which 5 were waited for; matrix products, arithmetic and copies ran while one was open for 4% of the time, Pallas kernels for 32%

profile of v1, /device:TPU:1, one launch (start us, length us, event | category | flops | bytes accessed | tf_op | source)
XLA Modules:
  0.0 129.7 jit_solution(6203367816912054736)
XLA Ops:
  0.7 1.3 fusion.1
  2.2 1.5 %collective-permute-start.3 = (bf16[256,256]{1,0:T(8,128)(2,1)S(1)}, bf16[256,256]{1,0:T(8,128)(2,1)S(1)}, u32[]{:S(2)}, u32[]{:S(2)}) collective-permute-start(bf16[256,256]{1,0:T(8,128)(2,1)S(1)} %broadcast_select_fusion.6), channel_id=1, source_target_pairs={{0,4},{4,0},{8,12},{12,8},{16,20},{20,16},{24,28},{28,24},{32,36},... | collective-permute-start | bytes 393224 | tf_op jit(solution)/shard_map/ppermute | solution.py:45
  4.8 2.9 %collective-permute-start.5 = (bf16[512,256]{1,0:T(8,128)(2,1)S(1)}, bf16[512,256]{1,0:T(8,128)(2,1)S(1)}, u32[]{:S(2)}, u32[]{:S(2)}) collective-permute-start(bf16[512,256]{1,0:T(8,128)(2,1)S(1)} %pad_maximum_fusion), channel_id=1, source_target_pairs={{0,96},{4,28},{8,104},{12,20},{16,112},{20,12},{24,120},{28,4},{32... | collective-permute-start | bytes 786440 | tf_op jit(solution)/shard_map/ppermute | solution.py:45
  7.8 4.1 %collective-permute-done.5 = bf16[512,256]{1,0:T(8,128)(2,1)S(1)} collective-permute-done((bf16[512,256]{1,0:T(8,128)(2,1)S(1)}, bf16[512,256]{1,0:T(8,128)(2,1)S(1)}, u32[]{:S(2)}, u32[]{:S(2)}) %collective-permute-start.5) | collective-permute-done | bytes 262176 | tf_op jit(solution)/shard_map/ppermute | solution.py:45
  11.8 1.4 %collective-permute-done.4 = bf16[512,256]{1,0:T(8,128)(2,1)S(1)} collective-permute-done((bf16[512,256]{1,0:T(8,128)(2,1)S(1)}, bf16[512,256]{1,0:T(8,128)(2,1)S(1)}, u32[]{:S(2)}, u32[]{:S(2)}) %collective-permute-start.4) | collective-permute-done | bytes 262176 | tf_op jit(solution)/shard_map/ppermute | solution.py:45
  13.3 4.0 %collective-permute-done.6 = bf16[512,256]{1,0:T(8,128)(2,1)S(1)} collective-permute-done((bf16[512,256]{1,0:T(8,128)(2,1)S(1)}, bf16[512,256]{1,0:T(8,128)(2,1)S(1)}, u32[]{:S(2)}, u32[]{:S(2)}) %collective-permute-start.6) | collective-permute-done | bytes 262176 | tf_op jit(solution)/shard_map/ppermute | solution.py:45
  17.4 2.6 %collective-permute-start.8 = (bf16[2048,256]{1,0:T(8,128)(2,1)S(1)}, bf16[2048,256]{1,0:T(8,128)(2,1)S(1)}, u32[]{:S(2)}, u32[]{:S(2)}) collective-permute-start(bf16[2048,256]{1,0:T(8,128)(2,1)S(1)} %constant_dynamic-update-slice_fusion.own), channel_id=1, source_target_pairs={{0,24},{4,100},{8,16},{12,108},{16,8},{20,116},{24,0},{28,124},{32... | collective-permute-start | bytes 3145736 | tf_op jit(solution)/shard_map/ppermute | solution.py:45
  19.9 1.0 select_bitcast_fusion
  21.0 1.4 %collective-permute-start = (bf16[2048,128]{1,0:T(8,128)(2,1)}, bf16[2048,128]{1,0:T(8,128)(2,1)}, u32[]{:S(2)}, u32[]{:S(2)}) collective-permute-start(bf16[2048,128]{1,0:T(8,128)(2,1)} %get-tuple-element.27), channel_id=1, source_target_pairs={{0,4},{8,12},{16,20},{24,28},{32,36},{40,44},{48,52},{56,60},{64,6... | collective-permute-start | bytes 1572872 | tf_op jit(solution)/shard_map/ppermute | solution.py:45
  22.4 9.2 %collective-permute-start.1 = (bf16[2048,128]{1,0:T(8,128)(2,1)}, bf16[2048,128]{1,0:T(8,128)(2,1)}, u32[]{:S(2)}, u32[]{:S(2)}) collective-permute-start(bf16[2048,128]{1,0:T(8,128)(2,1)} %get-tuple-element.27), channel_id=1, source_target_pairs={{4,120},{12,112},{20,104},{28,96},{36,88},{44,80},{52,72},{60,64},... | collective-permute-start | bytes 1572872 | tf_op jit(solution)/shard_map/ppermute | solution.py:45
  31.6 3.6 %collective-permute-start.2 = (bf16[2048,128]{1,0:T(8,128)(2,1)}, bf16[2048,128]{1,0:T(8,128)(2,1)}, u32[]{:S(2)}, u32[]{:S(2)}) collective-permute-start(bf16[2048,128]{1,0:T(8,128)(2,1)} %get-tuple-element.26), channel_id=1, source_target_pairs={{4,124},{12,116},{20,108},{28,100},{36,92},{44,84},{52,76},{60,68}... | collective-permute-start | bytes 1572872 | tf_op jit(solution)/shard_map/ppermute | solution.py:45
  36.0 1.1 broadcast_select_fusion.3.x_ref
  37.3 2.6 %collective-permute-start.10 = (bf16[1024,256]{1,0:T(8,128)(2,1)S(1)}, bf16[1024,256]{1,0:T(8,128)(2,1)S(1)}, u32[]{:S(2)}, u32[]{:S(2)}) collective-permute-start(bf16[1024,256]{1,0:T(8,128)(2,1)S(1)} %slice.37), channel_id=1, source_target_pairs={{0,24},{4,100},{8,16},{12,108},{16,8},{20,116},{24,0},{28,124},{32... | collective-permute-start | bytes 1572872 | tf_op jit(solution)/shard_map/ppermute | solution.py:45
  39.9 6.2 %collective-permute-done.2 = bf16[2048,128]{1,0:T(8,128)(2,1)} collective-permute-done((bf16[2048,128]{1,0:T(8,128)(2,1)}, bf16[2048,128]{1,0:T(8,128)(2,1)}, u32[]{:S(2)}, u32[]{:S(2)}) %collective-permute-start.2) | collective-permute-done | bytes 524320 | tf_op jit(solution)/shard_map/ppermute | solution.py:45
  46.0 1.1 broadcast_select_fusion.2.y_ref
  47.2 5.3 %shard_map.85 = (f32[2048,128]{1,0:T(8,128)S(1)}, f32[2048,128]{1,0:T(8,128)S(1)}, f32[2048,128]{1,0:T(8,128)S(1)}, f32[128,128]{1,0:T(8,128)S(1)}, f32[128,128]...) custom-call(s32[18]{0:T(128)S(1)} %pad_add_fusion.tab, ...), custom_call_target="tpu_custom_call" | custom-call | flops 2147483648 | bytes 1048576 | tf_op jit(solution)/shard_map/pallas_call | solution.py:258
  52.5 6.6 %shard_map.86 = (f32[2048,128]{1,0:T(8,128)S(1)}, f32[2048,128]{1,0:T(8,128)S(1)}, f32[2048,128]{1,0:T(8,128)S(1)}, f32[128,128]{1,0:T(8,128)S(1)}, f32[128,128]...) custom-call(s32[18]{0:T(128)S(1)} %pad_add_fusion.tab, ...), custom_call_target="tpu_custom_call" | custom-call | flops 2147483648 | bytes 1048576 | tf_op jit(solution)/shard_map/pallas_call | solution.py:258
  59.1 2.5 %shard_map.87 = (bf16[2048,128]{1,0:T(8,128)(2,1)S(1)}, bf16[2048,128]{1,0:T(8,128)(2,1)S(1)}) custom-call(s32[18]{0:T(128)S(1)} %pad_add_fusion.tab, bf16[1024,256]{1,0:T(8,128)(2,1)S(1)} %collective-permute-done.9.opp0, bf16[1024,256]{1,0:T(8,128)(2,1)S(1)} %collective-permute-done.10.opp1, bf16[64,128]{1,0:T(8,128)(2,1)S(1)} %dynamic-slice_bitcast_fusion.1.wk, ...), custom_call_target="tpu_custom_call" | custom-call | flops 1073741824 | bytes 1048576 | tf_op jit(solution)/shard_map/pallas_call | solution.py:258
  62.5 4.0 %collective-permute-start.13 = (bf16[2048,128]{1,0:T(8,128)(2,1)}, bf16[2048,128]{1,0:T(8,128)(2,1)S(1)}, u32[]{:S(2)}, u32[]{:S(2)}) collective-permute-start(bf16[2048,128]{1,0:T(8,128)(2,1)} %broadcast_select_fusion), channel_id=1, source_target_pairs={{0,124},{4,0},{8,116},{12,8},{16,108},{20,16},{24,100},{28,24},{32... | collective-permute-start | bytes 1572872 | tf_op jit(solution)/shard_map/ppermute | solution.py:45
  66.5 29.5 %shard_map.88 = (bf16[2048,128]{1,0:T(8,128)(2,1)S(1)}, bf16[2048,128]{1,0:T(8,128)(2,1)S(1)}, f32[128,1,128]{2,1,0:T(1,128)S(1)}) custom-call(s32[18]{0:T(128)S(1)} %pad_add_fusion.tab, bf16[2048,128]{1,0:T(8,128)(2,1)S(1)} %broadcast_select_fusion.3.x_ref, bf16[2048,128]{1,0:T(8,128)(2,1)S(1)} %broadcast_select_fusion.2.y_ref, ...), custom_call_target="tpu_custom_call" | custom-call | flops 9663676416 | bytes 1048576 | tf_op jit(solution)/shard_map/pallas_call | solution.py:258
  97.4 4.5 %collective-permute-start.12 = (bf16[2048,128]{1,0:T(8,128)(2,1)S(1)}, bf16[2048,128]{1,0:T(8,128)(2,1)}, u32[]{:S(2)}, u32[]{:S(2)}) collective-permute-start(bf16[2048,128]{1,0:T(8,128)(2,1)S(1)} %get-tuple-element.45), channel_id=1, source_target_pairs={{4,124},{12,116},{20,108},{28,100},{36,92},{44,84},{52,76},{60,68}... | collective-permute-start | bytes 1572872 | tf_op jit(solution)/shard_map/ppermute | solution.py:45
  101.9 4.1 %collective-permute-start.14 = (bf16[2048,128]{1,0:T(8,128)(2,1)S(1)}, bf16[2048,128]{1,0:T(8,128)(2,1)}, u32[]{:S(2)}, u32[]{:S(2)}) collective-permute-start(bf16[2048,128]{1,0:T(8,128)(2,1)S(1)} %get-tuple-element.43.sy_ref), channel_id=1, source_target_pairs={{4,124},{12,116},{20,108},{28,100},{36,92},{44,84},{52,76},{60,68}... | collective-permute-start | bytes 1572872 | tf_op jit(solution)/shard_map/ppermute | solution.py:45
  106.0 18.6 %all_to_all.5 = f32[128,1,128]{2,1,0:T(1,128)S(1)} all-to-all(f32[128,1,128]{2,1,0:T(1,128)S(1)} %get-tuple-element.48), channel_id=1, replica_groups=mesh['x'=4,'y'=4,'c'=2,'h'=4] {'x','y','c','h'}, dimensions={0} | all-to-all | bytes 131072 | tf_op jit(solution)/shard_map/all_to_all | solution.py:355
  126.0 2.6 %shard_map.89 = (bf16[256,16,128]{2,1,0:T(8,128)(2,1)}, bf16[256,16,128]{2,1,0:T(8,128)(2,1)}) custom-call(s32[18]{0:T(128)S(1)} %pad_add_fusion.tab, bf16[256,8,128]{2,1,0:T(8,128)(2,1)S(1)} %bitcast.29, bf16[256,8,128]{2,1,0:T(8,128)(2,1)S(1)} %bitcast.31, bf16[256,8,128]{2,1,0:T(8,128)(2,1)} %bitcast.15.refs_2_, bf16[256,8,128]{2,1,0:T(8,128)(2,1)S(1)} %bitcast.28, ...), custom_call_target="tpu_custom_call" | custom-call | bytes 1048576 | tf_op jit(solution)/shard_map/pallas_call | solution.py:258
  (55 shorter events, 5.5 us)
Async XLA Ops:
  0.6 35.2 %copy-start = (bf16[16,128,64]{1,2,0:T(8,128)(2,1)S(1)}, bf16[16,128,64]{1,2,0:T(8,128)(2,1)}, u32[]{:S(2)}) copy-start(bf16[16,128,64]{1,2,0:T(8,128)(2,1)} %param.9) | copy-start | bytes 786436
  2.2 2.4 %collective-permute-start.3 = (bf16[256,256]{1,0:T(8,128)(2,1)S(1)}, bf16[256,256]{1,0:T(8,128)(2,1)S(1)}, u32[]{:S(2)}, u32[]{:S(2)}) collective-permute-start(bf16[256,256]{1,0:T(8,128)(2,1)S(1)} %broadcast_select_fusion.6), channel_id=1, source_target_pairs={{0,4},{4,0},{8,12},{12,8},{16,20},{20,16},{24,28},{28,24},{32,36},... | collective-permute-start | bytes 393224 | tf_op jit(solution)/shard_map/ppermute | solution.py:45
  4.8 15.1 %copy-start.7 = (bf16[256,16,128]{2,1,0:T(8,128)(2,1)S(1)}, bf16[256,16,128]{2,1,0:T(8,128)(2,1)}, u32[]{:S(2)}) copy-start(bf16[256,16,128]{2,1,0:T(8,128)(2,1)} %param.6) | copy-start | bytes 3145732
  4.8 7.0 %collective-permute-start.5 = (bf16[512,256]{1,0:T(8,128)(2,1)S(1)}, bf16[512,256]{1,0:T(8,128)(2,1)S(1)}, u32[]{:S(2)}, u32[]{:S(2)}) collective-permute-start(bf16[512,256]{1,0:T(8,128)(2,1)S(1)} %pad_maximum_fusion), channel_id=1, source_target_pairs={{0,96},{4,28},{8,104},{12,20},{16,112},{20,12},{24,120},{28,4},{32... | collective-permute-start | bytes 786440 | tf_op jit(solution)/shard_map/ppermute | solution.py:45
  7.8 5.5 %collective-permute-start.4 = (bf16[512,256]{1,0:T(8,128)(2,1)S(1)}, bf16[512,256]{1,0:T(8,128)(2,1)S(1)}, u32[]{:S(2)}, u32[]{:S(2)}) collective-permute-start(bf16[512,256]{1,0:T(8,128)(2,1)S(1)} %pad_maximum_fusion), channel_id=1, source_target_pairs={{0,32},{4,12},{8,40},{12,4},{16,48},{20,28},{24,56},{28,20},{32,0}... | collective-permute-start | bytes 786440 | tf_op jit(solution)/shard_map/ppermute | solution.py:45
  11.8 5.5 %collective-permute-start.6 = (bf16[512,256]{1,0:T(8,128)(2,1)S(1)}, bf16[512,256]{1,0:T(8,128)(2,1)S(1)}, u32[]{:S(2)}, u32[]{:S(2)}) collective-permute-start(bf16[512,256]{1,0:T(8,128)(2,1)S(1)} %collective-permute-done.5), channel_id=1, source_target_pairs={{0,32},{4,12},{8,40},{12,4},{16,48},{20,28},{24,56},{28,20},{32,0}... | collective-permute-start | bytes 786440 | tf_op jit(solution)/shard_map/ppermute | solution.py:45
  17.4 29.8 %copy-start.5 = (bf16[2048,256]{1,0:T(8,128)(2,1)}, bf16[2048,256]{1,0:T(8,128)(2,1)S(1)}, u32[]{:S(2)}) copy-start(bf16[2048,256]{1,0:T(8,128)(2,1)S(1)} %constant_dynamic-update-slice_fusion.own) | copy-start | bytes 3145732
  17.4 19.7 %collective-permute-start.8 = (bf16[2048,256]{1,0:T(8,128)(2,1)S(1)}, bf16[2048,256]{1,0:T(8,128)(2,1)S(1)}, u32[]{:S(2)}, u32[]{:S(2)}) collective-permute-start(bf16[2048,256]{1,0:T(8,128)(2,1)S(1)} %constant_dynamic-update-slice_fusion.own), channel_id=1, source_target_pairs={{0,24},{4,100},{8,16},{12,108},{16,8},{20,116},{24,0},{28,124},{32... | collective-permute-start | bytes 3145736 | tf_op jit(solution)/shard_map/ppermute | solution.py:45
  19.9 17.3 %collective-permute-start.7 = (bf16[2048,256]{1,0:T(8,128)(2,1)S(1)}, bf16[2048,256]{1,0:T(8,128)(2,1)S(1)}, u32[]{:S(2)}, u32[]{:S(2)}) collective-permute-start(bf16[2048,256]{1,0:T(8,128)(2,1)S(1)} %constant_dynamic-update-slice_fusion.own), channel_id=1, source_target_pairs={{0,8},{4,36},{8,0},{12,44},{16,24},{20,52},{24,16},{28,60},{32,40}... | collective-permute-start | bytes 3145736 | tf_op jit(solution)/shard_map/ppermute | solution.py:45
  21.0 14.9 %copy-start.9 = (bf16[2,128,64]{1,2,0:T(8,128)(2,1)S(1)}, bf16[2,128,64]{1,2,0:T(8,128)(2,1)}, u32[]{:S(2)}) copy-start(bf16[2,128,64]{1,2,0:T(8,128)(2,1)} %param.10) | copy-start | bytes 98308
  21.0 15.0 %collective-permute-start = (bf16[2048,128]{1,0:T(8,128)(2,1)}, bf16[2048,128]{1,0:T(8,128)(2,1)}, u32[]{:S(2)}, u32[]{:S(2)}) collective-permute-start(bf16[2048,128]{1,0:T(8,128)(2,1)} %get-tuple-element.27), channel_id=1, source_target_pairs={{0,4},{8,12},{16,20},{24,28},{32,36},{40,44},{48,52},{56,60},{64,6... | collective-permute-start | bytes 1572872 | tf_op jit(solution)/shard_map/ppermute | solution.py:45
  22.4 23.6 %collective-permute-start.1 = (bf16[2048,128]{1,0:T(8,128)(2,1)}, bf16[2048,128]{1,0:T(8,128)(2,1)}, u32[]{:S(2)}, u32[]{:S(2)}) collective-permute-start(bf16[2048,128]{1,0:T(8,128)(2,1)} %get-tuple-element.27), channel_id=1, source_target_pairs={{4,120},{12,112},{20,104},{28,96},{36,88},{44,80},{52,72},{60,64},... | collective-permute-start | bytes 1572872 | tf_op jit(solution)/shard_map/ppermute | solution.py:45
  31.6 14.5 %collective-permute-start.2 = (bf16[2048,128]{1,0:T(8,128)(2,1)}, bf16[2048,128]{1,0:T(8,128)(2,1)}, u32[]{:S(2)}, u32[]{:S(2)}) collective-permute-start(bf16[2048,128]{1,0:T(8,128)(2,1)} %get-tuple-element.26), channel_id=1, source_target_pairs={{4,124},{12,116},{20,108},{28,100},{36,92},{44,84},{52,76},{60,68}... | collective-permute-start | bytes 1572872 | tf_op jit(solution)/shard_map/ppermute | solution.py:45
  37.1 15.4 %copy-start.1 = (bf16[2048,256]{1,0:T(8,128)(2,1)}, bf16[2048,256]{1,0:T(8,128)(2,1)S(1)}, u32[]{:S(2)}) copy-start(bf16[2048,256]{1,0:T(8,128)(2,1)S(1)} %collective-permute-done.8.right) | copy-start | bytes 3145732
  37.2 21.9 %collective-permute-start.9 = (bf16[1024,256]{1,0:T(8,128)(2,1)S(1)}, bf16[1024,256]{1,0:T(8,128)(2,1)S(1)}, u32[]{:S(2)}, u32[]{:S(2)}) collective-permute-start(bf16[1024,256]{1,0:T(8,128)(2,1)S(1)} %slice.36), channel_id=1, source_target_pairs={{0,8},{4,36},{8,0},{12,44},{16,24},{20,52},{24,16},{28,60},{32,40}... | collective-permute-start | bytes 1572872 | tf_op jit(solution)/shard_map/ppermute | solution.py:45
  37.3 15.2 %copy-start.3 = (bf16[2048,256]{1,0:T(8,128)(2,1)}, bf16[2048,256]{1,0:T(8,128)(2,1)S(1)}, u32[]{:S(2)}) copy-start(bf16[2048,256]{1,0:T(8,128)(2,1)S(1)} %collective-permute-done.7.left) | copy-start | bytes 3145732
  37.3 21.8 %collective-permute-start.10 = (bf16[1024,256]{1,0:T(8,128)(2,1)S(1)}, bf16[1024,256]{1,0:T(8,128)(2,1)S(1)}, u32[]{:S(2)}, u32[]{:S(2)}) collective-permute-start(bf16[1024,256]{1,0:T(8,128)(2,1)S(1)} %slice.37), channel_id=1, source_target_pairs={{0,24},{4,100},{8,16},{12,108},{16,8},{20,116},{24,0},{28,124},{32... | collective-permute-start | bytes 1572872 | tf_op jit(solution)/shard_map/ppermute | solution.py:45
  59.1 7.3 %copy-start.4 = (bf16[2048,256]{1,0:T(8,128)(2,1)S(1)}, bf16[2048,256]{1,0:T(8,128)(2,1)}, u32[]{:S(2)}) copy-start(bf16[2048,256]{1,0:T(8,128)(2,1)} %copy-done.3) | copy-start | bytes 3145732
  59.1 7.3 %copy-start.6 = (bf16[2048,256]{1,0:T(8,128)(2,1)S(1)}, bf16[2048,256]{1,0:T(8,128)(2,1)}, u32[]{:S(2)}) copy-start(bf16[2048,256]{1,0:T(8,128)(2,1)} %copy-done.5) | copy-start | bytes 3145732
  61.6 4.8 %copy-start.2 = (bf16[2048,256]{1,0:T(8,128)(2,1)S(1)}, bf16[2048,256]{1,0:T(8,128)(2,1)}, u32[]{:S(2)}) copy-start(bf16[2048,256]{1,0:T(8,128)(2,1)} %copy-done.1) | copy-start | bytes 3145732
  62.5 63.5 %collective-permute-start.13 = (bf16[2048,128]{1,0:T(8,128)(2,1)}, bf16[2048,128]{1,0:T(8,128)(2,1)S(1)}, u32[]{:S(2)}, u32[]{:S(2)}) collective-permute-start(bf16[2048,128]{1,0:T(8,128)(2,1)} %broadcast_select_fusion), channel_id=1, source_target_pairs={{0,124},{4,0},{8,116},{12,8},{16,108},{20,16},{24,100},{28,24},{32... | collective-permute-start | bytes 1572872 | tf_op jit(solution)/shard_map/ppermute | solution.py:45
  96.9 29.1 %collective-permute-start.11 = (bf16[2048,128]{1,0:T(8,128)(2,1)}, bf16[2048,128]{1,0:T(8,128)(2,1)S(1)}, u32[]{:S(2)}, u32[]{:S(2)}) collective-permute-start(bf16[2048,128]{1,0:T(8,128)(2,1)} %broadcast_select_fusion.1), channel_id=1, source_target_pairs={{0,124},{4,0},{8,116},{12,8},{16,108},{20,16},{24,100},{28,24},{32... | collective-permute-start | bytes 1572872 | tf_op jit(solution)/shard_map/ppermute | solution.py:45
  97.4 28.6 %collective-permute-start.12 = (bf16[2048,128]{1,0:T(8,128)(2,1)S(1)}, bf16[2048,128]{1,0:T(8,128)(2,1)}, u32[]{:S(2)}, u32[]{:S(2)}) collective-permute-start(bf16[2048,128]{1,0:T(8,128)(2,1)S(1)} %get-tuple-element.45), channel_id=1, source_target_pairs={{4,124},{12,116},{20,108},{28,100},{36,92},{44,84},{52,76},{60,68}... | collective-permute-start | bytes 1572872 | tf_op jit(solution)/shard_map/ppermute | solution.py:45
  101.9 24.1 %collective-permute-start.14 = (bf16[2048,128]{1,0:T(8,128)(2,1)S(1)}, bf16[2048,128]{1,0:T(8,128)(2,1)}, u32[]{:S(2)}, u32[]{:S(2)}) collective-permute-start(bf16[2048,128]{1,0:T(8,128)(2,1)S(1)} %get-tuple-element.43.sy_ref), channel_id=1, source_target_pairs={{4,124},{12,116},{20,108},{28,100},{36,92},{44,84},{52,76},{60,68}... | collective-permute-start | bytes 1572872 | tf_op jit(solution)/shard_map/ppermute | solution.py:45
  (1 other events, 1.3 us)

commit v2 on v1

--- a/solution.py
+++ b/solution.py
@@ -153,7 +153,7 @@
 
 def teacher_kernel(
     tab, x_ref, y_ref, own, left, right, opp0, opp1, sx_ref, sy_ref,
-    ox_ref, oy_ref, loss_ref, kv_s, part_ref, top_s, sum_s, acc_s, sems,
+    ox_ref, oy_ref, loss_ref, kv_s, q_s, part_ref, top_s, sum_s, acc_s, sems,
 ):
     chip = tab[16]
     far = 15 - chip
@@ -173,10 +173,18 @@
     unit = 1.4426950408889634 / 128**0.5
     part_ref[...] = jnp.zeros_like(part_ref)
 
-    def tile(q_ref, piece, k, v, diagonal, first):
+    for index, ref in enumerate((x_ref, y_ref)):
+        scaled = ref[...].astype(F32) * unit
+        high = scaled.astype(BF)
+        q_s[index, :, :128] = high
+        q_s[index, :, 128:] = (scaled - high.astype(F32)).astype(BF)
+
+    def tile(index, piece, place, diagonal, first):
         rows = slice(piece * SUB, (piece + 1) * SUB)
+        k, v = kv_s[place, :128], kv_s[place, 128:]
         wide = k.shape[0] // 128
-        s = lax.dot_general(q_ref[rows, :], k, NT, preferred_element_type=F32) * unit
+        twice = jnp.concatenate([k, k], axis=1)
+        s = lax.dot_general(q_s[index, rows, :], twice, NT, preferred_element_type=F32)
         if diagonal:
             shape = (SUB, BLK)
             row = (lax.broadcasted_iota(jnp.int32, shape, 0) >> 3) + piece * (SUB // 8)
@@ -198,18 +206,21 @@
             acc_s[rows, :] = acc_s[rows, :] * keep + mixed
         top_s[rows, :] = top
 
-    def segment(q_ref, k, v, count, s_ref, o_ref):
+    def both(index, place, diagonal=False, first=False):
         for piece in range(2):
-            tile(q_ref, piece, k, v, True, True)
-
+            tile(index, piece, place, diagonal, first)
+
+    def segment(index, count, s_ref, o_ref):
         def step(j, _):
-            place = block_at(j, 2 * BLK)
-            k, v = kv_s[place, :128], kv_s[place, 128:]
-            for piece in range(2):
-                tile(q_ref, piece, k, v, False, False)
+            both(index, block_at(j, 4 * BLK))
             return 0
 
-        lax.fori_loop(0, count, step, 0)
+        lax.fori_loop(0, count // 2, step, 0)
+
+        @pl.when(count % 2 == 1)
+        def _():
+            both(index, block_at(count - 1, 2 * BLK))
+
         for piece in range(2):
             rows = slice(piece * SUB, (piece + 1) * SUB)
             total = jnp.sum(sum_s[rows, :], axis=-1, keepdims=True)
@@ -218,17 +229,19 @@
             diff = out.astype(F32) - s_ref[rows, :].astype(F32)
             part_ref[...] += jnp.sum((diff * diff).reshape(SUB // 8, 8, 128), axis=0)
 
-    for copy in copies:
+    copies[0].wait()
+    both(0, block_at(chip * 2), True, True)
+    for copy in copies[1:]:
         copy.wait()
-    place = block_at(chip * 2)
-    segment(x_ref, kv_s[place, :128], kv_s[place, 128:], chip, sx_ref, ox_ref)
-    place = block_at(far, 2 * BLK)
-    segment(y_ref, kv_s[place, :128], kv_s[place, 128:], far, sy_ref, oy_ref)
+    segment(0, chip, sx_ref, ox_ref)
+    both(1, block_at(far, 2 * BLK), True, True)
+    segment(1, far, sy_ref, oy_ref)
     loss_ref[...] = jnp.full_like(loss_ref, jnp.sum(part_ref[...]))
 
 
 def assemble_kernel(tab, *refs):
-    sources, outs, sems = (refs[:3], refs[3:6]), refs[6:8], refs[8]
+    sources, parts, outs, loss_ref, sems = (refs[:3], refs[3:6]), refs[6], refs[7:9], *refs[9:]
+    loss_ref[0, 0] = jnp.sum(parts[...]) * (1.0 / (128 * outs[0].size * 128))
     for core in range(2):
 
         @pl.when(tab[17] == core)
@@ -245,7 +258,7 @@
                 copy.wait()
 
 
-def call(kernel, args, outs, scratch=(), flops=0, anywhere=(), limit=24, out_space=pltpu.VMEM):
+def call(kernel, args, outs, scratch=(), flops=0, anywhere=(), limit=24, out_space=None):
     vmem = pl.BlockSpec(memory_space=pltpu.VMEM)
     specs = [
         pl.BlockSpec(memory_space=pltpu.SMEM)
@@ -259,7 +272,7 @@
         kernel,
         out_shape=[jax.ShapeDtypeStruct(shape, kind) for shape, kind in outs],
         in_specs=specs,
-        out_specs=[pl.BlockSpec(memory_space=out_space)] * len(outs),
+        out_specs=[pl.BlockSpec(memory_space=m) for m in out_space or [pltpu.VMEM] * len(outs)],
         scratch_shapes=list(scratch),
         compiler_params=pltpu.CompilerParams(vmem_limit_bytes=limit << 20),
         cost_estimate=pl.CostEstimate(flops=flops, bytes_accessed=1 << 20, transcendentals=0),
@@ -343,7 +356,11 @@
         teacher_kernel,
         (table, x, y, own, left, right, opp0, opp1, sx, sy),
         [(many, BF)] * 2 + [((peers, 1, 128), F32)],
-        [pltpu.VMEM((16 * 2 * BLK, 256), BF), pltpu.VMEM((8, 128), F32)]
+        [
+            pltpu.VMEM((16 * 2 * BLK, 256), BF),
+            pltpu.VMEM((2, 2 * SUB, 256), BF),
+            pltpu.VMEM((8, 128), F32),
+        ]
         + [pltpu.VMEM((2 * SUB, 128), F32)] * 3
         + [pltpu.SemaphoreType.DMA((16,))],
         flops=9 << 30,
@@ -353,16 +370,15 @@
     teacher_parts = (ox, *send_back(ox, oy))
 
     parts = lax.all_to_all(part, SEQ + ("h",), 0, 0, tiled=True)
-    loss = jnp.sum(parts[:, 0, 0]) / (16 * 2 * rows * heads * lax.axis_size("h") * size)
-    parts = [p.reshape(rows, 8, size) for p in teacher_parts + student_parts]
-    teacher_attn, student_attn = call(
+    pieces = [p.reshape(rows, 8, size) for p in teacher_parts + student_parts]
+    teacher_attn, student_attn, loss = call(
         assemble_kernel,
-        (table, *parts),
-        [((rows, heads, size), BF)] * 2,
+        (table, *pieces, parts),
+        [((rows, heads, size), BF)] * 2 + [((1, 1), F32)],
         [pltpu.SemaphoreType.DMA((4,))],
-        out_space=pl.ANY,
-    )
-    return teacher_attn, student_attn, loss
+        out_space=[pl.ANY, pl.ANY, pltpu.SMEM],
+    )
+    return teacher_attn, student_attn, loss.reshape(())
 
 
 def solution(mesh):

time: 130 us -> 122 us (0.938)
  Pallas kernels: 46.5 us -> 42.5 us
  other arithmetic: 5.93 us -> 3.6 us
  between operations: 2.79 us -> 1.08 us
    pallas_call x5, Pallas kernels: 46.5 us -> 42.5 us  [call(): pl.pallas_call(kernel, out_shape=[jax.ShapeDtypeStruct(shape, kind) for s...]
    select_n x6, other arithmetic: 4.99 us -> 3.4 us  [body(): pick = lambda a, b: jnp.where(first, a, b)]
  transfers between devices with their start and end apart: 15 -> 15, of which waited for: 5 -> 5; matrix products, arithmetic and copies ran while one was open for 4% -> 3% of each run, Pallas kernels for 32% -> 31%
where the time goes in v2:
time: 122 us
  Pallas kernels  42.5 us (35%)
  starting transfers between devices  36.5 us (30%)
  blocking collectives  18.9 us (15%)
  waiting for transfers between devices  16.7 us (14%)
  other arithmetic  3.6 us (3%)
  local copies, waits for them, and re-layouts  2.36 us (2%)
    pallas_call x5, Pallas kernels, call(): pl.pallas_call(kernel, out_shape=[jax.ShapeDtypeStruct(shape, kind) for s...  42.5 us
    ppermute x15, starting transfers between devices, permute(): return lax.ppermute(value, axes, pairs)  36.5 us
    all_to_all x1, blocking collectives, body(): parts = lax.all_to_all(part, SEQ + ('h',), 0, 0, tiled=True)  18.9 us
    ppermute x15, waiting for transfers between devices, permute(): return lax.ppermute(value, axes, pairs)  16.7 us
    select_n x6, other arithmetic, body(): pick = lambda a, b: jnp.where(first, a, b)  3.4 us
  transfers between devices with their start and end apart: 15, of which 5 were waited for; matrix products, arithmetic and copies ran while one was open for 3% of the time, Pallas kernels for 31%

profile of v2, /device:TPU:1, one launch (start us, length us, event | category | flops | bytes accessed | tf_op | source)
XLA Modules:
  0.0 121.6 jit_solution(5937549362649311696)
XLA Ops:
  0.7 1.3 %fusion.1 = (bf16[256,1,128]{2,1,0:T(2,128)(2,1)S(1)}, bf16[256,1,128]{2,1,0:T(2,128)(2,1)S(1)}) fusion(bf16[256,2,128]{2,1,0:T(2,128)(2,1)} %param.7), kind=kLoop, calls=%fused_computation.27 | loop fusion | bytes 262144 | tf_op jit(solution)/shard_map/slice | solution.py:289
  2.2 1.5 %collective-permute-start.3 = (bf16[256,256]{1,0:T(8,128)(2,1)S(1)}, bf16[256,256]{1,0:T(8,128)(2,1)S(1)}, u32[]{:S(2)}, u32[]{:S(2)}) collective-permute-start(bf16[256,256]{1,0:T(8,128)(2,1)S(1)} %broadcast_select_fusion.6), channel_id=1, source_target_pairs={{0,4},{4,0},{8,12},{12,8},{16,20},{20,16},{24,28},{28,24},{32,36},... | collective-permute-start | bytes 393224 | tf_op jit(solution)/shard_map/ppermute | solution.py:45
  4.8 2.9 %collective-permute-start.5 = (bf16[512,256]{1,0:T(8,128)(2,1)S(1)}, bf16[512,256]{1,0:T(8,128)(2,1)S(1)}, u32[]{:S(2)}, u32[]{:S(2)}) collective-permute-start(bf16[512,256]{1,0:T(8,128)(2,1)S(1)} %pad_maximum_fusion), channel_id=1, source_target_pairs={{0,96},{4,28},{8,104},{12,20},{16,112},{20,12},{24,120},{28,4},{32... | collective-permute-start | bytes 786440 | tf_op jit(solution)/shard_map/ppermute | solution.py:45
  7.8 4.1 %collective-permute-done.5 = bf16[512,256]{1,0:T(8,128)(2,1)S(1)} collective-permute-done((bf16[512,256]{1,0:T(8,128)(2,1)S(1)}, bf16[512,256]{1,0:T(8,128)(2,1)S(1)}, u32[]{:S(2)}, u32[]{:S(2)}) %collective-permute-start.5) | collective-permute-done | bytes 262176 | tf_op jit(solution)/shard_map/ppermute | solution.py:45
  11.8 1.4 %collective-permute-done.4 = bf16[512,256]{1,0:T(8,128)(2,1)S(1)} collective-permute-done((bf16[512,256]{1,0:T(8,128)(2,1)S(1)}, bf16[512,256]{1,0:T(8,128)(2,1)S(1)}, u32[]{:S(2)}, u32[]{:S(2)}) %collective-permute-start.4) | collective-permute-done | bytes 262176 | tf_op jit(solution)/shard_map/ppermute | solution.py:45
  13.3 4.0 %collective-permute-done.6 = bf16[512,256]{1,0:T(8,128)(2,1)S(1)} collective-permute-done((bf16[512,256]{1,0:T(8,128)(2,1)S(1)}, bf16[512,256]{1,0:T(8,128)(2,1)S(1)}, u32[]{:S(2)}, u32[]{:S(2)}) %collective-permute-start.6) | collective-permute-done | bytes 262176 | tf_op jit(solution)/shard_map/ppermute | solution.py:45
  17.4 2.6 %collective-permute-start.8 = (bf16[2048,256]{1,0:T(8,128)(2,1)S(1)}, bf16[2048,256]{1,0:T(8,128)(2,1)S(1)}, u32[]{:S(2)}, u32[]{:S(2)}) collective-permute-start(bf16[2048,256]{1,0:T(8,128)(2,1)S(1)} %constant_dynamic-update-slice_fusion.own), channel_id=1, source_target_pairs={{0,24},{4,100},{8,16},{12,108},{16,8},{20,116},{24,0},{28,124},{32... | collective-permute-start | bytes 3145736 | tf_op jit(solution)/shard_map/ppermute | solution.py:45
  19.9 1.0 select_bitcast_fusion
  21.0 1.4 %collective-permute-start = (bf16[2048,128]{1,0:T(8,128)(2,1)}, bf16[2048,128]{1,0:T(8,128)(2,1)}, u32[]{:S(2)}, u32[]{:S(2)}) collective-permute-start(bf16[2048,128]{1,0:T(8,128)(2,1)} %get-tuple-element.28), channel_id=1, source_target_pairs={{0,4},{8,12},{16,20},{24,28},{32,36},{40,44},{48,52},{56,60},{64,6... | collective-permute-start | bytes 1572872 | tf_op jit(solution)/shard_map/ppermute | solution.py:45
  22.4 9.2 %collective-permute-start.1 = (bf16[2048,128]{1,0:T(8,128)(2,1)}, bf16[2048,128]{1,0:T(8,128)(2,1)}, u32[]{:S(2)}, u32[]{:S(2)}) collective-permute-start(bf16[2048,128]{1,0:T(8,128)(2,1)} %get-tuple-element.28), channel_id=1, source_target_pairs={{4,120},{12,112},{20,104},{28,96},{36,88},{44,80},{52,72},{60,64},... | collective-permute-start | bytes 1572872 | tf_op jit(solution)/shard_map/ppermute | solution.py:45
  31.6 3.5 %collective-permute-start.2 = (bf16[2048,128]{1,0:T(8,128)(2,1)}, bf16[2048,128]{1,0:T(8,128)(2,1)}, u32[]{:S(2)}, u32[]{:S(2)}) collective-permute-start(bf16[2048,128]{1,0:T(8,128)(2,1)} %get-tuple-element.27), channel_id=1, source_target_pairs={{4,124},{12,116},{20,108},{28,100},{36,92},{44,84},{52,76},{60,68}... | collective-permute-start | bytes 1572872 | tf_op jit(solution)/shard_map/ppermute | solution.py:45
  36.0 1.1 broadcast_select_fusion.3.x_ref
  37.3 2.6 %collective-permute-start.10 = (bf16[1024,256]{1,0:T(8,128)(2,1)S(1)}, bf16[1024,256]{1,0:T(8,128)(2,1)S(1)}, u32[]{:S(2)}, u32[]{:S(2)}) collective-permute-start(bf16[1024,256]{1,0:T(8,128)(2,1)S(1)} %slice.33), channel_id=1, source_target_pairs={{0,24},{4,100},{8,16},{12,108},{16,8},{20,116},{24,0},{28,124},{32... | collective-permute-start | bytes 1572872 | tf_op jit(solution)/shard_map/ppermute | solution.py:45
  39.9 6.2 %collective-permute-done.2 = bf16[2048,128]{1,0:T(8,128)(2,1)} collective-permute-done((bf16[2048,128]{1,0:T(8,128)(2,1)}, bf16[2048,128]{1,0:T(8,128)(2,1)}, u32[]{:S(2)}, u32[]{:S(2)}) %collective-permute-start.2) | collective-permute-done | bytes 524320 | tf_op jit(solution)/shard_map/ppermute | solution.py:45
  46.0 1.1 broadcast_select_fusion.2.y_ref
  47.1 5.3 %shard_map.85 = (f32[2048,128]{1,0:T(8,128)S(1)}, f32[2048,128]{1,0:T(8,128)S(1)}, f32[2048,128]{1,0:T(8,128)S(1)}, f32[128,128]{1,0:T(8,128)S(1)}, f32[128,128]...) custom-call(s32[18]{0:T(128)S(1)} %pad_add_fusion.tab, ...), custom_call_target="tpu_custom_call" | custom-call | flops 2147483648 | bytes 1048576 | tf_op jit(solution)/shard_map/pallas_call | solution.py:271
  52.4 6.6 %shard_map.86 = (f32[2048,128]{1,0:T(8,128)S(1)}, f32[2048,128]{1,0:T(8,128)S(1)}, f32[2048,128]{1,0:T(8,128)S(1)}, f32[128,128]{1,0:T(8,128)S(1)}, f32[128,128]...) custom-call(s32[18]{0:T(128)S(1)} %pad_add_fusion.tab, ...), custom_call_target="tpu_custom_call" | custom-call | flops 2147483648 | bytes 1048576 | tf_op jit(solution)/shard_map/pallas_call | solution.py:271
  59.1 2.5 %shard_map.87 = (bf16[2048,128]{1,0:T(8,128)(2,1)S(1)}, bf16[2048,128]{1,0:T(8,128)(2,1)S(1)}) custom-call(s32[18]{0:T(128)S(1)} %pad_add_fusion.tab, bf16[1024,256]{1,0:T(8,128)(2,1)S(1)} %collective-permute-done.9.opp0, bf16[1024,256]{1,0:T(8,128)(2,1)S(1)} %collective-permute-done.10.opp1, bf16[64,128]{1,0:T(8,128)(2,1)S(1)} %dynamic-slice_bitcast_fusion.1.wk, ...), custom_call_target="tpu_custom_call" | custom-call | flops 1073741824 | bytes 1048576 | tf_op jit(solution)/shard_map/pallas_call | solution.py:271
  61.6 4.0 %collective-permute-start.13 = (bf16[2048,128]{1,0:T(8,128)(2,1)S(1)}, bf16[2048,128]{1,0:T(8,128)(2,1)S(1)}, u32[]{:S(2)}, u32[]{:S(2)}) collective-permute-start(bf16[2048,128]{1,0:T(8,128)(2,1)S(1)} %broadcast_select_fusion), channel_id=1, source_target_pairs={{0,124},{4,0},{8,116},{12,8},{16,108},{20,16},{24,100},{28,24},{32... | collective-permute-start | bytes 1572872 | tf_op jit(solution)/shard_map/ppermute | solution.py:45
  65.6 25.4 %shard_map.88 = (bf16[2048,128]{1,0:T(8,128)(2,1)S(1)}, bf16[2048,128]{1,0:T(8,128)(2,1)S(1)}, f32[128,1,128]{2,1,0:T(1,128)S(1)}) custom-call(s32[18]{0:T(128)S(1)} %pad_add_fusion.tab, bf16[2048,128]{1,0:T(8,128)(2,1)S(1)} %broadcast_select_fusion.3.x_ref, bf16[2048,128]{1,0:T(8,128)(2,1)S(1)} %broadcast_select_fusion.2.y_ref, ...), custom_call_target="tpu_custom_call" | custom-call | flops 9663676416 | bytes 1048576 | tf_op jit(solution)/shard_map/pallas_call | solution.py:271
  91.2 4.5 %collective-permute-start.12 = (bf16[2048,128]{1,0:T(8,128)(2,1)S(1)}, bf16[2048,128]{1,0:T(8,128)(2,1)S(1)}, u32[]{:S(2)}, u32[]{:S(2)}) collective-permute-start(bf16[2048,128]{1,0:T(8,128)(2,1)S(1)} %get-tuple-element.46), channel_id=1, source_target_pairs={{4,124},{12,116},{20,108},{28,100},{36,92},{44,84},{52,76},{60,68}... | collective-permute-start | bytes 1572872 | tf_op jit(solution)/shard_map/ppermute | solution.py:45
  95.8 4.1 %collective-permute-start.14 = (bf16[2048,128]{1,0:T(8,128)(2,1)S(1)}, bf16[2048,128]{1,0:T(8,128)(2,1)S(1)}, u32[]{:S(2)}, u32[]{:S(2)}) collective-permute-start(bf16[2048,128]{1,0:T(8,128)(2,1)S(1)} %get-tuple-element.44.sy_ref), channel_id=1, source_target_pairs={{4,124},{12,116},{20,108},{28,100},{36,92},{44,84},{52,76},{60,68}... | collective-permute-start | bytes 1572872 | tf_op jit(solution)/shard_map/ppermute | solution.py:45
  99.8 18.9 %all_to_all.5.refs_6_ = f32[128,1,128]{2,1,0:T(1,128)S(1)} all-to-all(f32[128,1,128]{2,1,0:T(1,128)S(1)} %get-tuple-element.47), channel_id=1, replica_groups=mesh['x'=4,'y'=4,'c'=2,'h'=4] {'x','y','c','h'}, dimensions={0} | all-to-all | bytes 131072 | tf_op jit(solution)/shard_map/all_to_all | solution.py:372
  118.7 2.7 %shard_map.89 = (bf16[256,16,128]{2,1,0:T(8,128)(2,1)}, bf16[256,16,128]{2,1,0:T(8,128)(2,1)}, f32[1,1]{1,0:T(1,128)}) custom-call(s32[18]{0:T(128)S(1)} %pad_add_fusion.tab, bf16[256,8,128]{2,1,0:T(8,128)(2,1)S(1)} %bitcast.30, bf16[256,8,128]{2,1,0:T(8,128)(2,1)S(1)} %bitcast.32, bf16[256,8,128]{2,1,0:T(8,128)(2,1)S(1)} %bitcast.33, ...), custom_call_target="tpu_custom_call" | custom-call | bytes 1048576 | tf_op jit(solution)/shard_map/pallas_call | solution.py:271
  (42 shorter events, 2.7 us)
Async XLA Ops:
  0.6 35.3 %copy-start = (bf16[16,128,64]{1,2,0:T(8,128)(2,1)S(1)}, bf16[16,128,64]{1,2,0:T(8,128)(2,1)}, u32[]{:S(2)}) copy-start(bf16[16,128,64]{1,2,0:T(8,128)(2,1)} %param.9) | copy-start | bytes 786436
  0.7 1.3 %copy-start.2 = (bf16[256,2,128]{2,1,0:T(2,128)(2,1)S(1)}, bf16[256,2,128]{2,1,0:T(2,128)(2,1)}, u32[]{:S(2)}) copy-start(bf16[256,2,128]{2,1,0:T(2,128)(2,1)} %param.8) | copy-start | bytes 393220
  2.2 2.4 %collective-permute-start.3 = (bf16[256,256]{1,0:T(8,128)(2,1)S(1)}, bf16[256,256]{1,0:T(8,128)(2,1)S(1)}, u32[]{:S(2)}, u32[]{:S(2)}) collective-permute-start(bf16[256,256]{1,0:T(8,128)(2,1)S(1)} %broadcast_select_fusion.6), channel_id=1, source_target_pairs={{0,4},{4,0},{8,12},{12,8},{16,20},{20,16},{24,28},{28,24},{32,36},... | collective-permute-start | bytes 393224 | tf_op jit(solution)/shard_map/ppermute | solution.py:45
  4.8 15.1 %copy-start.1 = (bf16[256,16,128]{2,1,0:T(8,128)(2,1)S(1)}, bf16[256,16,128]{2,1,0:T(8,128)(2,1)}, u32[]{:S(2)}) copy-start(bf16[256,16,128]{2,1,0:T(8,128)(2,1)} %param.6) | copy-start | bytes 3145732
  4.8 7.0 %collective-permute-start.5 = (bf16[512,256]{1,0:T(8,128)(2,1)S(1)}, bf16[512,256]{1,0:T(8,128)(2,1)S(1)}, u32[]{:S(2)}, u32[]{:S(2)}) collective-permute-start(bf16[512,256]{1,0:T(8,128)(2,1)S(1)} %pad_maximum_fusion), channel_id=1, source_target_pairs={{0,96},{4,28},{8,104},{12,20},{16,112},{20,12},{24,120},{28,4},{32... | collective-permute-start | bytes 786440 | tf_op jit(solution)/shard_map/ppermute | solution.py:45
  7.8 5.5 %collective-permute-start.4 = (bf16[512,256]{1,0:T(8,128)(2,1)S(1)}, bf16[512,256]{1,0:T(8,128)(2,1)S(1)}, u32[]{:S(2)}, u32[]{:S(2)}) collective-permute-start(bf16[512,256]{1,0:T(8,128)(2,1)S(1)} %pad_maximum_fusion), channel_id=1, source_target_pairs={{0,32},{4,12},{8,40},{12,4},{16,48},{20,28},{24,56},{28,20},{32,0}... | collective-permute-start | bytes 786440 | tf_op jit(solution)/shard_map/ppermute | solution.py:45
  11.8 5.5 %collective-permute-start.6 = (bf16[512,256]{1,0:T(8,128)(2,1)S(1)}, bf16[512,256]{1,0:T(8,128)(2,1)S(1)}, u32[]{:S(2)}, u32[]{:S(2)}) collective-permute-start(bf16[512,256]{1,0:T(8,128)(2,1)S(1)} %collective-permute-done.5), channel_id=1, source_target_pairs={{0,32},{4,12},{8,40},{12,4},{16,48},{20,28},{24,56},{28,20},{32,0}... | collective-permute-start | bytes 786440 | tf_op jit(solution)/shard_map/ppermute | solution.py:45
  17.4 19.7 %collective-permute-start.8 = (bf16[2048,256]{1,0:T(8,128)(2,1)S(1)}, bf16[2048,256]{1,0:T(8,128)(2,1)S(1)}, u32[]{:S(2)}, u32[]{:S(2)}) collective-permute-start(bf16[2048,256]{1,0:T(8,128)(2,1)S(1)} %constant_dynamic-update-slice_fusion.own), channel_id=1, source_target_pairs={{0,24},{4,100},{8,16},{12,108},{16,8},{20,116},{24,0},{28,124},{32... | collective-permute-start | bytes 3145736 | tf_op jit(solution)/shard_map/ppermute | solution.py:45
  19.9 17.3 %collective-permute-start.7 = (bf16[2048,256]{1,0:T(8,128)(2,1)S(1)}, bf16[2048,256]{1,0:T(8,128)(2,1)S(1)}, u32[]{:S(2)}, u32[]{:S(2)}) collective-permute-start(bf16[2048,256]{1,0:T(8,128)(2,1)S(1)} %constant_dynamic-update-slice_fusion.own), channel_id=1, source_target_pairs={{0,8},{4,36},{8,0},{12,44},{16,24},{20,52},{24,16},{28,60},{32,40}... | collective-permute-start | bytes 3145736 | tf_op jit(solution)/shard_map/ppermute | solution.py:45
  21.0 14.9 %copy-start.3 = (bf16[2,128,64]{1,2,0:T(8,128)(2,1)S(1)}, bf16[2,128,64]{1,2,0:T(8,128)(2,1)}, u32[]{:S(2)}) copy-start(bf16[2,128,64]{1,2,0:T(8,128)(2,1)} %param.10) | copy-start | bytes 98308
  21.0 15.0 %collective-permute-start = (bf16[2048,128]{1,0:T(8,128)(2,1)}, bf16[2048,128]{1,0:T(8,128)(2,1)}, u32[]{:S(2)}, u32[]{:S(2)}) collective-permute-start(bf16[2048,128]{1,0:T(8,128)(2,1)} %get-tuple-element.28), channel_id=1, source_target_pairs={{0,4},{8,12},{16,20},{24,28},{32,36},{40,44},{48,52},{56,60},{64,6... | collective-permute-start | bytes 1572872 | tf_op jit(solution)/shard_map/ppermute | solution.py:45
  22.4 23.6 %collective-permute-start.1 = (bf16[2048,128]{1,0:T(8,128)(2,1)}, bf16[2048,128]{1,0:T(8,128)(2,1)}, u32[]{:S(2)}, u32[]{:S(2)}) collective-permute-start(bf16[2048,128]{1,0:T(8,128)(2,1)} %get-tuple-element.28), channel_id=1, source_target_pairs={{4,120},{12,112},{20,104},{28,96},{36,88},{44,80},{52,72},{60,64},... | collective-permute-start | bytes 1572872 | tf_op jit(solution)/shard_map/ppermute | solution.py:45
  31.6 14.4 %collective-permute-start.2 = (bf16[2048,128]{1,0:T(8,128)(2,1)}, bf16[2048,128]{1,0:T(8,128)(2,1)}, u32[]{:S(2)}, u32[]{:S(2)}) collective-permute-start(bf16[2048,128]{1,0:T(8,128)(2,1)} %get-tuple-element.27), channel_id=1, source_target_pairs={{4,124},{12,116},{20,108},{28,100},{36,92},{44,84},{52,76},{60,68}... | collective-permute-start | bytes 1572872 | tf_op jit(solution)/shard_map/ppermute | solution.py:45
  37.2 21.9 %collective-permute-start.9 = (bf16[1024,256]{1,0:T(8,128)(2,1)S(1)}, bf16[1024,256]{1,0:T(8,128)(2,1)S(1)}, u32[]{:S(2)}, u32[]{:S(2)}) collective-permute-start(bf16[1024,256]{1,0:T(8,128)(2,1)S(1)} %slice.32), channel_id=1, source_target_pairs={{0,8},{4,36},{8,0},{12,44},{16,24},{20,52},{24,16},{28,60},{32,40}... | collective-permute-start | bytes 1572872 | tf_op jit(solution)/shard_map/ppermute | solution.py:45
  37.3 21.8 %collective-permute-start.10 = (bf16[1024,256]{1,0:T(8,128)(2,1)S(1)}, bf16[1024,256]{1,0:T(8,128)(2,1)S(1)}, u32[]{:S(2)}, u32[]{:S(2)}) collective-permute-start(bf16[1024,256]{1,0:T(8,128)(2,1)S(1)} %slice.33), channel_id=1, source_target_pairs={{0,24},{4,100},{8,16},{12,108},{16,8},{20,116},{24,0},{28,124},{32... | collective-permute-start | bytes 1572872 | tf_op jit(solution)/shard_map/ppermute | solution.py:45
  61.6 57.1 %collective-permute-start.13 = (bf16[2048,128]{1,0:T(8,128)(2,1)S(1)}, bf16[2048,128]{1,0:T(8,128)(2,1)S(1)}, u32[]{:S(2)}, u32[]{:S(2)}) collective-permute-start(bf16[2048,128]{1,0:T(8,128)(2,1)S(1)} %broadcast_select_fusion), channel_id=1, source_target_pairs={{0,124},{4,0},{8,116},{12,8},{16,108},{20,16},{24,100},{28,24},{32... | collective-permute-start | bytes 1572872 | tf_op jit(solution)/shard_map/ppermute | solution.py:45
  91.1 27.6 %collective-permute-start.11 = (bf16[2048,128]{1,0:T(8,128)(2,1)S(1)}, bf16[2048,128]{1,0:T(8,128)(2,1)S(1)}, u32[]{:S(2)}, u32[]{:S(2)}) collective-permute-start(bf16[2048,128]{1,0:T(8,128)(2,1)S(1)} %broadcast_select_fusion.1), channel_id=1, source_target_pairs={{0,124},{4,0},{8,116},{12,8},{16,108},{20,16},{24,100},{28,24},{32... | collective-permute-start | bytes 1572872 | tf_op jit(solution)/shard_map/ppermute | solution.py:45
  91.2 27.5 %collective-permute-start.12 = (bf16[2048,128]{1,0:T(8,128)(2,1)S(1)}, bf16[2048,128]{1,0:T(8,128)(2,1)S(1)}, u32[]{:S(2)}, u32[]{:S(2)}) collective-permute-start(bf16[2048,128]{1,0:T(8,128)(2,1)S(1)} %get-tuple-element.46), channel_id=1, source_target_pairs={{4,124},{12,116},{20,108},{28,100},{36,92},{44,84},{52,76},{60,68}... | collective-permute-start | bytes 1572872 | tf_op jit(solution)/shard_map/ppermute | solution.py:45
  95.8 23.0 %collective-permute-start.14 = (bf16[2048,128]{1,0:T(8,128)(2,1)S(1)}, bf16[2048,128]{1,0:T(8,128)(2,1)S(1)}, u32[]{:S(2)}, u32[]{:S(2)}) collective-permute-start(bf16[2048,128]{1,0:T(8,128)(2,1)S(1)} %get-tuple-element.44.sy_ref), channel_id=1, source_target_pairs={{4,124},{12,116},{20,108},{28,100},{36,92},{44,84},{52,76},{60,68}... | collective-permute-start | bytes 1572872 | tf_op jit(solution)/shard_map/ppermute | solution.py:45

commit v3 on v2

--- a/solution.py
+++ b/solution.py
@@ -13,7 +13,7 @@
 F32 = jnp.float32
 NT = (((1,), (1,)), ((), ()))
 BLK = 256
-SUB = 1024
+SUB = 2048
 
 MASKS = (0, 1, 3, 2)
 
@@ -207,7 +207,7 @@
         top_s[rows, :] = top
 
     def both(index, place, diagonal=False, first=False):
-        for piece in range(2):
+        for piece in range(8 * BLK // SUB):
             tile(index, piece, place, diagonal, first)
 
     def segment(index, count, s_ref, o_ref):
@@ -221,7 +221,7 @@
         def _():
             both(index, block_at(count - 1, 2 * BLK))
 
-        for piece in range(2):
+        for piece in range(8 * BLK // SUB):
             rows = slice(piece * SUB, (piece + 1) * SUB)
             total = jnp.sum(sum_s[rows, :], axis=-1, keepdims=True)
             out = (acc_s[rows, :] / total).astype(BF)
@@ -358,10 +358,10 @@
         [(many, BF)] * 2 + [((peers, 1, 128), F32)],
         [
             pltpu.VMEM((16 * 2 * BLK, 256), BF),
-            pltpu.VMEM((2, 2 * SUB, 256), BF),
+            pltpu.VMEM((2, SUB, 256), BF),
             pltpu.VMEM((8, 128), F32),
         ]
-        + [pltpu.VMEM((2 * SUB, 128), F32)] * 3
+        + [pltpu.VMEM((SUB, 128), F32)] * 3
         + [pltpu.SemaphoreType.DMA((16,))],
         flops=9 << 30,
         anywhere=(3, 4, 5, 6, 7),

time: 122 us -> 122 us (level)
  no operation moved by 1% of the time
where the time goes in v3:
time: 122 us; the launch traced here: 121 us
  Pallas kernels  42.1 us (35%)
  starting transfers between devices  36.5 us (30%)
  blocking collectives  18.9 us (15%)
  waiting for transfers between devices  16.7 us (14%)
  other arithmetic  3.6 us (3%)
  local copies, waits for them, and re-layouts  2.36 us (2%)
    pallas_call x5, Pallas kernels, call(): pl.pallas_call(kernel, out_shape=[jax.ShapeDtypeStruct(shape, kind) for s...  42.1 us
    ppermute x15, starting transfers between devices, permute(): return lax.ppermute(value, axes, pairs)  36.5 us
    all_to_all x1, blocking collectives, body(): parts = lax.all_to_all(part, SEQ + ('h',), 0, 0, tiled=True)  18.9 us
    ppermute x15, waiting for transfers between devices, permute(): return lax.ppermute(value, axes, pairs)  16.7 us
    select_n x6, other arithmetic, body(): pick = lambda a, b: jnp.where(first, a, b)  3.4 us
  transfers between devices with their start and end apart: 15, of which 5 were waited for; matrix products, arithmetic and copies ran while one was open for 3% of the time, Pallas kernels for 31%

profile of v3, /device:TPU:1, one launch (start us, length us, event | category | flops | bytes accessed | tf_op | source)
XLA Modules:
  0.0 121.3 jit_solution(374932543879449569)
XLA Ops:
  0.7 1.3 %fusion.1 = (bf16[256,1,128]{2,1,0:T(2,128)(2,1)S(1)}, bf16[256,1,128]{2,1,0:T(2,128)(2,1)S(1)}) fusion(bf16[256,2,128]{2,1,0:T(2,128)(2,1)} %param.7), kind=kLoop, calls=%fused_computation.27 | loop fusion | bytes 262144 | tf_op jit(solution)/shard_map/slice | solution.py:289
  2.2 1.5 %collective-permute-start.3 = (bf16[256,256]{1,0:T(8,128)(2,1)S(1)}, bf16[256,256]{1,0:T(8,128)(2,1)S(1)}, u32[]{:S(2)}, u32[]{:S(2)}) collective-permute-start(bf16[256,256]{1,0:T(8,128)(2,1)S(1)} %broadcast_select_fusion.6), channel_id=1, source_target_pairs={{0,4},{4,0},{8,12},{12,8},{16,20},{20,16},{24,28},{28,24},{32,36},... | collective-permute-start | bytes 393224 | tf_op jit(solution)/shard_map/ppermute | solution.py:45
  4.8 2.9 %collective-permute-start.5 = (bf16[512,256]{1,0:T(8,128)(2,1)S(1)}, bf16[512,256]{1,0:T(8,128)(2,1)S(1)}, u32[]{:S(2)}, u32[]{:S(2)}) collective-permute-start(bf16[512,256]{1,0:T(8,128)(2,1)S(1)} %pad_maximum_fusion), channel_id=1, source_target_pairs={{0,96},{4,28},{8,104},{12,20},{16,112},{20,12},{24,120},{28,4},{32... | collective-permute-start | bytes 786440 | tf_op jit(solution)/shard_map/ppermute | solution.py:45
  7.8 4.1 %collective-permute-done.5 = bf16[512,256]{1,0:T(8,128)(2,1)S(1)} collective-permute-done((bf16[512,256]{1,0:T(8,128)(2,1)S(1)}, bf16[512,256]{1,0:T(8,128)(2,1)S(1)}, u32[]{:S(2)}, u32[]{:S(2)}) %collective-permute-start.5) | collective-permute-done | bytes 262176 | tf_op jit(solution)/shard_map/ppermute | solution.py:45
  11.8 1.4 %collective-permute-done.4 = bf16[512,256]{1,0:T(8,128)(2,1)S(1)} collective-permute-done((bf16[512,256]{1,0:T(8,128)(2,1)S(1)}, bf16[512,256]{1,0:T(8,128)(2,1)S(1)}, u32[]{:S(2)}, u32[]{:S(2)}) %collective-permute-start.4) | collective-permute-done | bytes 262176 | tf_op jit(solution)/shard_map/ppermute | solution.py:45
  13.3 4.0 %collective-permute-done.6 = bf16[512,256]{1,0:T(8,128)(2,1)S(1)} collective-permute-done((bf16[512,256]{1,0:T(8,128)(2,1)S(1)}, bf16[512,256]{1,0:T(8,128)(2,1)S(1)}, u32[]{:S(2)}, u32[]{:S(2)}) %collective-permute-start.6) | collective-permute-done | bytes 262176 | tf_op jit(solution)/shard_map/ppermute | solution.py:45
  17.4 2.6 %collective-permute-start.8 = (bf16[2048,256]{1,0:T(8,128)(2,1)S(1)}, bf16[2048,256]{1,0:T(8,128)(2,1)S(1)}, u32[]{:S(2)}, u32[]{:S(2)}) collective-permute-start(bf16[2048,256]{1,0:T(8,128)(2,1)S(1)} %constant_dynamic-update-slice_fusion.own), channel_id=1, source_target_pairs={{0,24},{4,100},{8,16},{12,108},{16,8},{20,116},{24,0},{28,124},{32... | collective-permute-start | bytes 3145736 | tf_op jit(solution)/shard_map/ppermute | solution.py:45
  19.9 1.0 select_bitcast_fusion
  21.0 1.4 %collective-permute-start = (bf16[2048,128]{1,0:T(8,128)(2,1)}, bf16[2048,128]{1,0:T(8,128)(2,1)}, u32[]{:S(2)}, u32[]{:S(2)}) collective-permute-start(bf16[2048,128]{1,0:T(8,128)(2,1)} %get-tuple-element.28), channel_id=1, source_target_pairs={{0,4},{8,12},{16,20},{24,28},{32,36},{40,44},{48,52},{56,60},{64,6... | collective-permute-start | bytes 1572872 | tf_op jit(solution)/shard_map/ppermute | solution.py:45
  22.4 9.2 %collective-permute-start.1 = (bf16[2048,128]{1,0:T(8,128)(2,1)}, bf16[2048,128]{1,0:T(8,128)(2,1)}, u32[]{:S(2)}, u32[]{:S(2)}) collective-permute-start(bf16[2048,128]{1,0:T(8,128)(2,1)} %get-tuple-element.28), channel_id=1, source_target_pairs={{4,120},{12,112},{20,104},{28,96},{36,88},{44,80},{52,72},{60,64},... | collective-permute-start | bytes 1572872 | tf_op jit(solution)/shard_map/ppermute | solution.py:45
  31.6 3.5 %collective-permute-start.2 = (bf16[2048,128]{1,0:T(8,128)(2,1)}, bf16[2048,128]{1,0:T(8,128)(2,1)}, u32[]{:S(2)}, u32[]{:S(2)}) collective-permute-start(bf16[2048,128]{1,0:T(8,128)(2,1)} %get-tuple-element.27), channel_id=1, source_target_pairs={{4,124},{12,116},{20,108},{28,100},{36,92},{44,84},{52,76},{60,68}... | collective-permute-start | bytes 1572872 | tf_op jit(solution)/shard_map/ppermute | solution.py:45
  36.0 1.1 broadcast_select_fusion.3.x_ref
  37.3 2.6 %collective-permute-start.10 = (bf16[1024,256]{1,0:T(8,128)(2,1)S(1)}, bf16[1024,256]{1,0:T(8,128)(2,1)S(1)}, u32[]{:S(2)}, u32[]{:S(2)}) collective-permute-start(bf16[1024,256]{1,0:T(8,128)(2,1)S(1)} %slice.33), channel_id=1, source_target_pairs={{0,24},{4,100},{8,16},{12,108},{16,8},{20,116},{24,0},{28,124},{32... | collective-permute-start | bytes 1572872 | tf_op jit(solution)/shard_map/ppermute | solution.py:45
  39.9 6.2 %collective-permute-done.2 = bf16[2048,128]{1,0:T(8,128)(2,1)} collective-permute-done((bf16[2048,128]{1,0:T(8,128)(2,1)}, bf16[2048,128]{1,0:T(8,128)(2,1)}, u32[]{:S(2)}, u32[]{:S(2)}) %collective-permute-start.2) | collective-permute-done | bytes 524320 | tf_op jit(solution)/shard_map/ppermute | solution.py:45
  46.0 1.1 broadcast_select_fusion.2.y_ref
  47.1 5.3 %shard_map.85 = (f32[2048,128]{1,0:T(8,128)S(1)}, f32[2048,128]{1,0:T(8,128)S(1)}, f32[2048,128]{1,0:T(8,128)S(1)}, f32[128,128]{1,0:T(8,128)S(1)}, f32[128,128]...) custom-call(s32[18]{0:T(128)S(1)} %pad_add_fusion.tab, ...), custom_call_target="tpu_custom_call" | custom-call | flops 2147483648 | bytes 1048576 | tf_op jit(solution)/shard_map/pallas_call | solution.py:271
  52.4 6.6 %shard_map.86 = (f32[2048,128]{1,0:T(8,128)S(1)}, f32[2048,128]{1,0:T(8,128)S(1)}, f32[2048,128]{1,0:T(8,128)S(1)}, f32[128,128]{1,0:T(8,128)S(1)}, f32[128,128]...) custom-call(s32[18]{0:T(128)S(1)} %pad_add_fusion.tab, ...), custom_call_target="tpu_custom_call" | custom-call | flops 2147483648 | bytes 1048576 | tf_op jit(solution)/shard_map/pallas_call | solution.py:271
  59.1 2.5 %shard_map.87 = (bf16[2048,128]{1,0:T(8,128)(2,1)S(1)}, bf16[2048,128]{1,0:T(8,128)(2,1)S(1)}) custom-call(s32[18]{0:T(128)S(1)} %pad_add_fusion.tab, bf16[1024,256]{1,0:T(8,128)(2,1)S(1)} %collective-permute-done.9.opp0, bf16[1024,256]{1,0:T(8,128)(2,1)S(1)} %collective-permute-done.10.opp1, bf16[64,128]{1,0:T(8,128)(2,1)S(1)} %dynamic-slice_bitcast_fusion.1.wk, ...), custom_call_target="tpu_custom_call" | custom-call | flops 1073741824 | bytes 1048576 | tf_op jit(solution)/shard_map/pallas_call | solution.py:271
  61.6 4.0 %collective-permute-start.13 = (bf16[2048,128]{1,0:T(8,128)(2,1)S(1)}, bf16[2048,128]{1,0:T(8,128)(2,1)S(1)}, u32[]{:S(2)}, u32[]{:S(2)}) collective-permute-start(bf16[2048,128]{1,0:T(8,128)(2,1)S(1)} %broadcast_select_fusion), channel_id=1, source_target_pairs={{0,124},{4,0},{8,116},{12,8},{16,108},{20,16},{24,100},{28,24},{32... | collective-permute-start | bytes 1572872 | tf_op jit(solution)/shard_map/ppermute | solution.py:45
  65.6 25.1 %shard_map.88 = (bf16[2048,128]{1,0:T(8,128)(2,1)S(1)}, bf16[2048,128]{1,0:T(8,128)(2,1)S(1)}, f32[128,1,128]{2,1,0:T(1,128)S(1)}) custom-call(s32[18]{0:T(128)S(1)} %pad_add_fusion.tab, bf16[2048,128]{1,0:T(8,128)(2,1)S(1)} %broadcast_select_fusion.3.x_ref, bf16[2048,128]{1,0:T(8,128)(2,1)S(1)} %broadcast_select_fusion.2.y_ref, ...), custom_call_target="tpu_custom_call" | custom-call | flops 9663676416 | bytes 1048576 | tf_op jit(solution)/shard_map/pallas_call | solution.py:271
  90.9 4.5 %collective-permute-start.12 = (bf16[2048,128]{1,0:T(8,128)(2,1)S(1)}, bf16[2048,128]{1,0:T(8,128)(2,1)S(1)}, u32[]{:S(2)}, u32[]{:S(2)}) collective-permute-start(bf16[2048,128]{1,0:T(8,128)(2,1)S(1)} %get-tuple-element.46), channel_id=1, source_target_pairs={{4,124},{12,116},{20,108},{28,100},{36,92},{44,84},{52,76},{60,68}... | collective-permute-start | bytes 1572872 | tf_op jit(solution)/shard_map/ppermute | solution.py:45
  95.5 4.1 %collective-permute-start.14 = (bf16[2048,128]{1,0:T(8,128)(2,1)S(1)}, bf16[2048,128]{1,0:T(8,128)(2,1)S(1)}, u32[]{:S(2)}, u32[]{:S(2)}) collective-permute-start(bf16[2048,128]{1,0:T(8,128)(2,1)S(1)} %get-tuple-element.44.sy_ref), channel_id=1, source_target_pairs={{4,124},{12,116},{20,108},{28,100},{36,92},{44,84},{52,76},{60,68}... | collective-permute-start | bytes 1572872 | tf_op jit(solution)/shard_map/ppermute | solution.py:45
  99.5 18.9 %all_to_all.5.refs_6_ = f32[128,1,128]{2,1,0:T(1,128)S(1)} all-to-all(f32[128,1,128]{2,1,0:T(1,128)S(1)} %get-tuple-element.47), channel_id=1, replica_groups=mesh['x'=4,'y'=4,'c'=2,'h'=4] {'x','y','c','h'}, dimensions={0} | all-to-all | bytes 131072 | tf_op jit(solution)/shard_map/all_to_all | solution.py:372
  118.4 2.7 %shard_map.89 = (bf16[256,16,128]{2,1,0:T(8,128)(2,1)}, bf16[256,16,128]{2,1,0:T(8,128)(2,1)}, f32[1,1]{1,0:T(1,128)}) custom-call(s32[18]{0:T(128)S(1)} %pad_add_fusion.tab, bf16[256,8,128]{2,1,0:T(8,128)(2,1)S(1)} %bitcast.30, bf16[256,8,128]{2,1,0:T(8,128)(2,1)S(1)} %bitcast.32, bf16[256,8,128]{2,1,0:T(8,128)(2,1)S(1)} %bitcast.33, ...), custom_call_target="tpu_custom_call" | custom-call | bytes 1048576 | tf_op jit(solution)/shard_map/pallas_call | solution.py:271
  (42 shorter events, 2.7 us)
Async XLA Ops:
  0.6 35.3 %copy-start = (bf16[16,128,64]{1,2,0:T(8,128)(2,1)S(1)}, bf16[16,128,64]{1,2,0:T(8,128)(2,1)}, u32[]{:S(2)}) copy-start(bf16[16,128,64]{1,2,0:T(8,128)(2,1)} %param.9) | copy-start | bytes 786436
  0.7 1.3 %copy-start.2 = (bf16[256,2,128]{2,1,0:T(2,128)(2,1)S(1)}, bf16[256,2,128]{2,1,0:T(2,128)(2,1)}, u32[]{:S(2)}) copy-start(bf16[256,2,128]{2,1,0:T(2,128)(2,1)} %param.8) | copy-start | bytes 393220
  2.2 2.4 %collective-permute-start.3 = (bf16[256,256]{1,0:T(8,128)(2,1)S(1)}, bf16[256,256]{1,0:T(8,128)(2,1)S(1)}, u32[]{:S(2)}, u32[]{:S(2)}) collective-permute-start(bf16[256,256]{1,0:T(8,128)(2,1)S(1)} %broadcast_select_fusion.6), channel_id=1, source_target_pairs={{0,4},{4,0},{8,12},{12,8},{16,20},{20,16},{24,28},{28,24},{32,36},... | collective-permute-start | bytes 393224 | tf_op jit(solution)/shard_map/ppermute | solution.py:45
  4.8 15.1 %copy-start.1 = (bf16[256,16,128]{2,1,0:T(8,128)(2,1)S(1)}, bf16[256,16,128]{2,1,0:T(8,128)(2,1)}, u32[]{:S(2)}) copy-start(bf16[256,16,128]{2,1,0:T(8,128)(2,1)} %param.6) | copy-start | bytes 3145732
  4.8 7.0 %collective-permute-start.5 = (bf16[512,256]{1,0:T(8,128)(2,1)S(1)}, bf16[512,256]{1,0:T(8,128)(2,1)S(1)}, u32[]{:S(2)}, u32[]{:S(2)}) collective-permute-start(bf16[512,256]{1,0:T(8,128)(2,1)S(1)} %pad_maximum_fusion), channel_id=1, source_target_pairs={{0,96},{4,28},{8,104},{12,20},{16,112},{20,12},{24,120},{28,4},{32... | collective-permute-start | bytes 786440 | tf_op jit(solution)/shard_map/ppermute | solution.py:45
  7.8 5.5 %collective-permute-start.4 = (bf16[512,256]{1,0:T(8,128)(2,1)S(1)}, bf16[512,256]{1,0:T(8,128)(2,1)S(1)}, u32[]{:S(2)}, u32[]{:S(2)}) collective-permute-start(bf16[512,256]{1,0:T(8,128)(2,1)S(1)} %pad_maximum_fusion), channel_id=1, source_target_pairs={{0,32},{4,12},{8,40},{12,4},{16,48},{20,28},{24,56},{28,20},{32,0}... | collective-permute-start | bytes 786440 | tf_op jit(solution)/shard_map/ppermute | solution.py:45
  11.8 5.5 %collective-permute-start.6 = (bf16[512,256]{1,0:T(8,128)(2,1)S(1)}, bf16[512,256]{1,0:T(8,128)(2,1)S(1)}, u32[]{:S(2)}, u32[]{:S(2)}) collective-permute-start(bf16[512,256]{1,0:T(8,128)(2,1)S(1)} %collective-permute-done.5), channel_id=1, source_target_pairs={{0,32},{4,12},{8,40},{12,4},{16,48},{20,28},{24,56},{28,20},{32,0}... | collective-permute-start | bytes 786440 | tf_op jit(solution)/shard_map/ppermute | solution.py:45
  17.4 19.7 %collective-permute-start.8 = (bf16[2048,256]{1,0:T(8,128)(2,1)S(1)}, bf16[2048,256]{1,0:T(8,128)(2,1)S(1)}, u32[]{:S(2)}, u32[]{:S(2)}) collective-permute-start(bf16[2048,256]{1,0:T(8,128)(2,1)S(1)} %constant_dynamic-update-slice_fusion.own), channel_id=1, source_target_pairs={{0,24},{4,100},{8,16},{12,108},{16,8},{20,116},{24,0},{28,124},{32... | collective-permute-start | bytes 3145736 | tf_op jit(solution)/shard_map/ppermute | solution.py:45
  19.9 17.3 %collective-permute-start.7 = (bf16[2048,256]{1,0:T(8,128)(2,1)S(1)}, bf16[2048,256]{1,0:T(8,128)(2,1)S(1)}, u32[]{:S(2)}, u32[]{:S(2)}) collective-permute-start(bf16[2048,256]{1,0:T(8,128)(2,1)S(1)} %constant_dynamic-update-slice_fusion.own), channel_id=1, source_target_pairs={{0,8},{4,36},{8,0},{12,44},{16,24},{20,52},{24,16},{28,60},{32,40}... | collective-permute-start | bytes 3145736 | tf_op jit(solution)/shard_map/ppermute | solution.py:45
  21.0 14.9 %copy-start.3 = (bf16[2,128,64]{1,2,0:T(8,128)(2,1)S(1)}, bf16[2,128,64]{1,2,0:T(8,128)(2,1)}, u32[]{:S(2)}) copy-start(bf16[2,128,64]{1,2,0:T(8,128)(2,1)} %param.10) | copy-start | bytes 98308
  21.0 15.0 %collective-permute-start = (bf16[2048,128]{1,0:T(8,128)(2,1)}, bf16[2048,128]{1,0:T(8,128)(2,1)}, u32[]{:S(2)}, u32[]{:S(2)}) collective-permute-start(bf16[2048,128]{1,0:T(8,128)(2,1)} %get-tuple-element.28), channel_id=1, source_target_pairs={{0,4},{8,12},{16,20},{24,28},{32,36},{40,44},{48,52},{56,60},{64,6... | collective-permute-start | bytes 1572872 | tf_op jit(solution)/shard_map/ppermute | solution.py:45
  22.4 23.6 %collective-permute-start.1 = (bf16[2048,128]{1,0:T(8,128)(2,1)}, bf16[2048,128]{1,0:T(8,128)(2,1)}, u32[]{:S(2)}, u32[]{:S(2)}) collective-permute-start(bf16[2048,128]{1,0:T(8,128)(2,1)} %get-tuple-element.28), channel_id=1, source_target_pairs={{4,120},{12,112},{20,104},{28,96},{36,88},{44,80},{52,72},{60,64},... | collective-permute-start | bytes 1572872 | tf_op jit(solution)/shard_map/ppermute | solution.py:45
  31.6 14.4 %collective-permute-start.2 = (bf16[2048,128]{1,0:T(8,128)(2,1)}, bf16[2048,128]{1,0:T(8,128)(2,1)}, u32[]{:S(2)}, u32[]{:S(2)}) collective-permute-start(bf16[2048,128]{1,0:T(8,128)(2,1)} %get-tuple-element.27), channel_id=1, source_target_pairs={{4,124},{12,116},{20,108},{28,100},{36,92},{44,84},{52,76},{60,68}... | collective-permute-start | bytes 1572872 | tf_op jit(solution)/shard_map/ppermute | solution.py:45
  37.2 21.9 %collective-permute-start.9 = (bf16[1024,256]{1,0:T(8,128)(2,1)S(1)}, bf16[1024,256]{1,0:T(8,128)(2,1)S(1)}, u32[]{:S(2)}, u32[]{:S(2)}) collective-permute-start(bf16[1024,256]{1,0:T(8,128)(2,1)S(1)} %slice.32), channel_id=1, source_target_pairs={{0,8},{4,36},{8,0},{12,44},{16,24},{20,52},{24,16},{28,60},{32,40}... | collective-permute-start | bytes 1572872 | tf_op jit(solution)/shard_map/ppermute | solution.py:45
  37.3 21.8 %collective-permute-start.10 = (bf16[1024,256]{1,0:T(8,128)(2,1)S(1)}, bf16[1024,256]{1,0:T(8,128)(2,1)S(1)}, u32[]{:S(2)}, u32[]{:S(2)}) collective-permute-start(bf16[1024,256]{1,0:T(8,128)(2,1)S(1)} %slice.33), channel_id=1, source_target_pairs={{0,24},{4,100},{8,16},{12,108},{16,8},{20,116},{24,0},{28,124},{32... | collective-permute-start | bytes 1572872 | tf_op jit(solution)/shard_map/ppermute | solution.py:45
  61.6 56.8 %collective-permute-start.13 = (bf16[2048,128]{1,0:T(8,128)(2,1)S(1)}, bf16[2048,128]{1,0:T(8,128)(2,1)S(1)}, u32[]{:S(2)}, u32[]{:S(2)}) collective-permute-start(bf16[2048,128]{1,0:T(8,128)(2,1)S(1)} %broadcast_select_fusion), channel_id=1, source_target_pairs={{0,124},{4,0},{8,116},{12,8},{16,108},{20,16},{24,100},{28,24},{32... | collective-permute-start | bytes 1572872 | tf_op jit(solution)/shard_map/ppermute | solution.py:45
  90.8 27.6 %collective-permute-start.11 = (bf16[2048,128]{1,0:T(8,128)(2,1)S(1)}, bf16[2048,128]{1,0:T(8,128)(2,1)S(1)}, u32[]{:S(2)}, u32[]{:S(2)}) collective-permute-start(bf16[2048,128]{1,0:T(8,128)(2,1)S(1)} %broadcast_select_fusion.1), channel_id=1, source_target_pairs={{0,124},{4,0},{8,116},{12,8},{16,108},{20,16},{24,100},{28,24},{32... | collective-permute-start | bytes 1572872 | tf_op jit(solution)/shard_map/ppermute | solution.py:45
  90.9 27.5 %collective-permute-start.12 = (bf16[2048,128]{1,0:T(8,128)(2,1)S(1)}, bf16[2048,128]{1,0:T(8,128)(2,1)S(1)}, u32[]{:S(2)}, u32[]{:S(2)}) collective-permute-start(bf16[2048,128]{1,0:T(8,128)(2,1)S(1)} %get-tuple-element.46), channel_id=1, source_target_pairs={{4,124},{12,116},{20,108},{28,100},{36,92},{44,84},{52,76},{60,68}... | collective-permute-start | bytes 1572872 | tf_op jit(solution)/shard_map/ppermute | solution.py:45
  95.5 23.0 %collective-permute-start.14 = (bf16[2048,128]{1,0:T(8,128)(2,1)S(1)}, bf16[2048,128]{1,0:T(8,128)(2,1)S(1)}, u32[]{:S(2)}, u32[]{:S(2)}) collective-permute-start(bf16[2048,128]{1,0:T(8,128)(2,1)S(1)} %get-tuple-element.44.sy_ref), channel_id=1, source_target_pairs={{4,124},{12,116},{20,108},{28,100},{36,92},{44,84},{52,76},{60,68}... | collective-permute-start | bytes 1572872 | tf_op jit(solution)/shard_map/ppermute | solution.py:45
